TPU v7x, 512 devices: a whole 4x8x8 slice. The times are simulated.
512 devices in a mesh: dp: 16 (over z, core), expert: 32 (over x, y).
Axes of the slice: x: 4, y: 8, z: 8, core: 2. Of those that a mesh axis runs over, the one named last changes fastest.
Arguments:
- tokens: bfloat16 [65536, 1664], P(('dp', 'expert')), may hold values from -6 to 6
- cotangent: bfloat16 [65536, 1664], P(('dp', 'expert')), may hold values from -6 to 6
- counts: int32 [65536], P(('dp', 'expert')), may hold values from 0 to 8
- picks: int32 [16, 32, 32], P('dp'), may hold values from 0 to 4095, as said below
- router: float32 [1664, 32], replicated, may hold values from -1 to 1
- w_in: bfloat16 [32, 1664, 4096], P('expert', None, 'dp'), may hold values from -0.15625 to 0.15625
- w_out: bfloat16 [32, 4096, 1664], P('expert', 'dp'), may hold values from -0.09375 to 0.09375
Outputs:
- grad_tokens: bfloat16 [65536, 1664], P(('dp', 'expert'))
- grad_w_in: bfloat16 [32, 1664, 4096], P('expert', None, 'dp')
- grad_w_out: bfloat16 [32, 4096, 1664], P('expert', 'dp')
- grad_router: float32 [1664, 32], replicated
Inputs may be any that keep to these rules, and one draw needn't show every extreme that they name: For each group and each expert, 32 distinct positions in increasing order; positions k * 128 to (k + 1) * 128 - 1 hold at most 2 of one expert's picks, and each expert takes exactly 2 from some such range in every group.
All inputs are finite; a program needn't handle non-finite values.
Results may differ from a plain program's by a relative error of at most 0.017.
Values may be sent and summed in bfloat16 or wider, within the bound.
No kernel may reach another device: no remote copies, remote signals or barrier semaphores. Data moves between devices by JAX's collectives and lax.ppermute only.
A program may use at most 64 MiB of HBM per device.

v0:
```python
import jax
import jax.numpy as jnp
from jax import lax
from jax.sharding import PartitionSpec as P


SLOT = 2


def dot_rows(left, right):
    return lax.dot_general(
        left, right, (((0,), (0,)), ((), ())), preferred_element_type=jnp.float32
    )


def dot_cols(left, right):
    return lax.dot_general(
        left, right, (((1,), (1,)), ((), ())), preferred_element_type=jnp.float32
    )


def dot_plain(left, right):
    return jnp.dot(left, right, preferred_element_type=jnp.float32)


def split_bf16(values, pieces):
    parts = []
    rest = values
    for _ in range(pieces):
        head = lax.reduce_precision(rest, 8, 7)
        parts.append(head.astype(jnp.bfloat16))
        rest = rest - head
    return parts


def one_hot(index, width):
    lanes = lax.broadcasted_iota(jnp.int32, (index.shape[0], width), 1)
    return (lanes == index[:, None]).astype(jnp.bfloat16)


def grads(tokens, cotangent, counts, picks, router, w_in, w_out):
    experts = lax.axis_size("expert")
    groups = lax.axis_size("dp")
    me = lax.axis_index("expert")
    tok_count, width = tokens.shape
    plan = picks[0]
    cap = plan.shape[1]
    block_in = w_in[0]
    block_out = w_out[0]

    low = me * tok_count
    inside = (plan >= low) & (plan < low + tok_count)
    held = jnp.sum(inside.astype(jnp.int32), axis=1)
    first = jnp.min(jnp.where(inside, plan, low + tok_count), axis=1) - low
    last = jnp.max(jnp.where(inside, plan, low - 1), axis=1) - low
    slot_a = jnp.where(held > 0, first, -1)
    slot_b = jnp.where(held > 1, last, -1)

    weight = jnp.maximum(counts, 1).astype(jnp.float32)
    scaled = (cotangent.astype(jnp.float32) / weight[:, None]).astype(jnp.bfloat16)
    none = jnp.full_like(slot_a, -1)
    pick_x = one_hot(jnp.stack([slot_a, slot_b, none, none], axis=1).reshape(-1), tok_count)
    pick_dy = one_hot(jnp.stack([none, none, slot_a, slot_b], axis=1).reshape(-1), tok_count)
    send = dot_plain(pick_x, tokens) + dot_plain(pick_dy, scaled)
    send = send.astype(jnp.bfloat16).reshape(experts, 2 * SLOT, width)
    recv = lax.all_to_all(send, "expert", split_axis=0, concat_axis=0, tiled=True)
    recv = recv.reshape(experts * 2 * SLOT, width)

    mine = lax.dynamic_index_in_dim(plan, me, 0, keepdims=False)
    owner = mine // tok_count
    rank = jnp.concatenate(
        [jnp.zeros((1,), jnp.int32), (owner[1:] == owner[:-1]).astype(jnp.int32)]
    )
    place_x = owner * (2 * SLOT) + rank
    pack = one_hot(jnp.concatenate([place_x, place_x + SLOT]), experts * 2 * SLOT)
    slab = dot_plain(pack, recv).astype(jnp.bfloat16)
    chips = groups // 2
    here = lax.axis_index("dp") // 2
    shape = (chips, cap, width)
    blocks = jnp.zeros((2,) + shape, jnp.bfloat16)
    up = down = slab
    for step in range(chips // 2 + 1):
        arrived = []
        if step == 0:
            arrived.append((slab, here))
        else:
            up = lax.ppermute(up, "dp", [(i, (i + 2) % groups) for i in range(groups)])
            arrived.append((up, (here - step) % chips))
            if step < chips // 2:
                down = lax.ppermute(down, "dp", [(i, (i - 2) % groups) for i in range(groups)])
                arrived.append((down, (here + step) % chips))
        for block, spot in arrived:
            block = block.reshape(2, 1, cap, width)
            blocks = lax.dynamic_update_slice(blocks, block, (0, spot, 0, 0))
    swap = [(i, i ^ 1) for i in range(groups)]
    own = blocks.reshape(2 * chips * cap, width)
    other = lax.ppermute(own, "dp", swap)
    own_x, own_dy = own[: chips * cap], own[chips * cap :]
    other_x, other_dy = other[: chips * cap], other[chips * cap :]

    router_parts = split_bf16(router, 3)
    router_wide = jnp.concatenate(router_parts, axis=1)
    router_back = jnp.concatenate([router_parts[0], router_parts[0], router_parts[1]], axis=1)
    mark = (lax.broadcasted_iota(jnp.int32, (1, experts), 1) == me).astype(jnp.float32)

    def hidden_grads(rows_x, rows_dy):
        logit_parts = dot_plain(rows_x, router_wide)
        logits = (
            logit_parts[:, 2 * experts :] + logit_parts[:, experts : 2 * experts]
        ) + logit_parts[:, :experts]
        prob = jax.nn.softmax(logits, axis=-1)
        gate = jnp.sum(prob * mark, axis=-1, keepdims=True)
        pre = dot_plain(rows_x, block_in)
        cdf = 0.5 * (1.0 + lax.erf(pre * 0.7071067811865476))
        slope = cdf + pre * jnp.exp(-0.5 * pre * pre) * 0.3989422804014327
        act = (pre * cdf).astype(jnp.bfloat16)
        dy_hidden = dot_cols(rows_dy, block_out)
        gate_part = jnp.sum(act.astype(jnp.float32) * dy_hidden, axis=-1, keepdims=True)
        pre_grad = (gate * dy_hidden * slope).astype(jnp.bfloat16)
        gated = (gate * act.astype(jnp.float32)).astype(jnp.bfloat16)
        return pre_grad, gated, (gate_part * gate) * (mark - prob)

    tiles = width // 128
    deal = experts * tiles // groups

    def row_grads(pre_grad, share_hi, share_lo, extra):
        left = jnp.concatenate([share_hi, share_lo, share_hi], axis=1)
        rows = dot_cols(pre_grad, block_in) + dot_cols(left, router_back)
        return jnp.concatenate([rows, extra], axis=1)

    other_pre, other_gated, other_share = hidden_grads(other_x, other_dy)
    own_pre, own_gated, own_share = hidden_grads(own_x, own_dy)
    own_hi, own_lo = split_bf16(own_share, 2)
    other_hi, other_lo = split_bf16(other_share, 2)
    router_part = dot_rows(own_hi, own_x) + dot_rows(own_lo, own_x)
    router_part += dot_rows(other_hi, other_x) + dot_rows(other_lo, other_x)
    router_part = router_part.astype(jnp.bfloat16)
    router_part = jnp.concatenate(
        [router_part[:, 128 * tile : 128 * (tile + 1)] for tile in range(tiles)]
    )
    core = lax.axis_index("dp") % 2
    row_id = jnp.arange(chips * cap, dtype=jnp.int32)

    def dealt(side):
        unit = (2 * (row_id // cap) + side) * deal + row_id % cap
        pick = one_hot(jnp.where(row_id % cap < deal, unit, -1), experts * tiles)
        return dot_plain(pick, router_part)

    own_extra, other_extra = dealt(core), dealt(1 - core)

    other_rows = row_grads(other_pre, other_hi, other_lo, other_extra)
    partner_rows = lax.ppermute(other_rows.astype(jnp.bfloat16), "dp", swap)
    own_rows = row_grads(own_pre, own_hi, own_lo, own_extra)
    own_rows = own_rows + partner_rows.astype(jnp.float32)
    columns = [[i for i in range(groups) if i % 2 == side] for side in range(2)]
    pieces = lax.all_to_all(
        own_rows.astype(jnp.bfloat16).reshape(chips, cap, width + 128),
        "dp",
        split_axis=0,
        concat_axis=0,
        axis_index_groups=columns,
        tiled=True,
    )
    pieces = jnp.sum(pieces.astype(jnp.float32), axis=0)
    row_sum = pieces[:, :width].astype(jnp.bfloat16)
    router_rows = pieces[:deal, width:].reshape(SLOT, width)

    grad_in = (dot_rows(own_x, own_pre) + dot_rows(other_x, other_pre)).astype(jnp.bfloat16)
    grad_out = (dot_rows(own_gated, own_dy) + dot_rows(other_gated, other_dy)).astype(jnp.bfloat16)

    slot = lax.broadcasted_iota(jnp.int32, (experts * 2 * SLOT, 1), 0) % (2 * SLOT)
    back_rows = dot_rows(one_hot(place_x, experts * 2 * SLOT), row_sum)
    for part in range(SLOT):
        back_rows += jnp.where(slot == SLOT + part, router_rows[part : part + 1], 0.0)
    ret = lax.all_to_all(
        back_rows.astype(jnp.bfloat16).reshape(experts, 2 * SLOT, width),
        "expert",
        split_axis=0,
        concat_axis=0,
        tiled=True,
    ).reshape(experts * 2 * SLOT, width)
    grad_tokens = dot_rows(pick_x, ret).astype(jnp.bfloat16)
    spot = lax.broadcasted_iota(jnp.int32, (SLOT, experts * 2 * SLOT), 1)
    line = lax.broadcasted_iota(jnp.int32, (SLOT, experts * 2 * SLOT), 0)
    router_rows = dot_plain((spot % (2 * SLOT) == SLOT + line).astype(jnp.bfloat16), ret)
    router_rows = jnp.broadcast_to(router_rows[None], (groups, SLOT, width))
    router_rows = lax.all_to_all(router_rows, "dp", split_axis=0, concat_axis=0, tiled=True)
    router_rows = router_rows.reshape(tiles, experts, 128)
    grad_router = jnp.swapaxes(router_rows, 0, 1).reshape(experts, width).T
    return grad_tokens, grad_in[None], grad_out[None], grad_router


def solution(mesh):
    placed = (
        P(("dp", "expert"), None),
        P(("dp", "expert"), None),
        P(("dp", "expert")),
        P("dp", None, None),
        P(),
        P("expert", None, "dp"),
        P("expert", "dp", None),
    )
    return jax.shard_map(
        grads,
        mesh=mesh,
        in_specs=placed,
        out_specs=(
            P(("dp", "expert"), None),
            P("expert", None, "dp"),
            P("expert", "dp", None),
            P(),
        ),
        check_vma=False,
    )
```

profile of v0, /device:TPU:1, one launch (start us, length us, event | category | flops | bytes accessed | tf_op | source)
XLA Modules:
  0.0 168.2 jit_solution(9543889938286482918)
XLA Ops:
  0.7 0.9 fusion.90
  2.7 1.3 fusion.67
  4.0 1.4 fusion.6
  5.4 0.9 reshape.236
  6.3 10.5 %all-to-all-start = ((bf16[32,4,1664]{2,1,0:T(4,128)(2,1)}), bf16[32,4,1664]{2,1,0:T(4,128)(2,1)S(1)}, u32[]{:S(2)}, u32[]{:S(2)}) async-start(bf16[32,4,1664]{2,1,0:T(4,128)(2,1)} %reshape.236), calls=%async_computation | async-start | bytes 851968 | tf_op jit(solution)/shard_map/all_to_all | solution.py:66
  16.9 0.7 and_select_fusion.4
  17.7 0.8 broadcast_add_fusion.1
  18.5 0.7 reduce-precision_convert_fusion
  19.3 9.8 %all-to-all-done = bf16[32,4,1664]{2,1,0:T(4,128)(2,1)S(1)} async-done(((bf16[32,4,1664]{2,1,0:T(4,128)(2,1)}), bf16[32,4,1664]{2,1,0:T(4,128)(2,1)S(1)}, u32[]{:S(2)}, u32[]{:S(2)}) %all-to-all-start) | async-done | bytes 426016 | tf_op jit(solution)/shard_map/all_to_all | solution.py:66
  29.5 4.0 %collective-permute-start = (bf16[64,1664]{1,0:T(8,128)(2,1)S(1)}, bf16[64,1664]{1,0:T(8,128)(2,1)S(1)}, u32[]{:S(2)}, u32[]{:S(2)}) collective-permute-start(bf16[64,1664]{1,0:T(8,128)(2,1)S(1)} %convolution_convert_fusion.1), channel_id=1, source_target_pairs={{0,64},{32,96},{64,128},{96,160},{128,192},{160,224},{192,256},{22... | collective-permute-start | bytes 638984 | tf_op jit(solution)/shard_map/ppermute | solution.py:87
  33.5 8.6 %collective-permute-start.1 = (bf16[64,1664]{1,0:T(8,128)(2,1)S(1)}, bf16[64,1664]{1,0:T(8,128)(2,1)S(1)}, u32[]{:S(2)}, u32[]{:S(2)}) collective-permute-start(bf16[64,1664]{1,0:T(8,128)(2,1)S(1)} %convolution_convert_fusion.1), channel_id=1, source_target_pairs={{0,448},{32,480},{64,0},{96,32},{128,64},{160,96},{192,128},{224,1... | collective-permute-start | bytes 638984 | tf_op jit(solution)/shard_map/ppermute | solution.py:90
  42.1 1.3 broadcast_in_dim.78
  43.4 0.7 constant_dynamic-update-slice_fusion.20
  44.1 1.9 %collective-permute-start.2 = (bf16[64,1664]{1,0:T(8,128)(2,1)S(1)}, bf16[64,1664]{1,0:T(8,128)(2,1)S(1)}, u32[]{:S(2)}, u32[]{:S(2)}) collective-permute-start(bf16[64,1664]{1,0:T(8,128)(2,1)S(1)} %collective-permute-done), channel_id=1, source_target_pairs={{0,64},{32,96},{64,128},{96,160},{128,192},{160,224},{192,256},{22... | collective-permute-start | bytes 638984 | tf_op jit(solution)/shard_map/ppermute | solution.py:87
  46.0 0.7 constant_dynamic-update-slice_fusion.19
  46.7 4.6 %collective-permute-start.3 = (bf16[64,1664]{1,0:T(8,128)(2,1)S(1)}, bf16[64,1664]{1,0:T(8,128)(2,1)S(1)}, u32[]{:S(2)}, u32[]{:S(2)}) collective-permute-start(bf16[64,1664]{1,0:T(8,128)(2,1)S(1)} %collective-permute-done.1), channel_id=1, source_target_pairs={{0,448},{32,480},{64,0},{96,32},{128,64},{160,96},{192,128},{224,1... | collective-permute-start | bytes 638984 | tf_op jit(solution)/shard_map/ppermute | solution.py:90
  51.3 0.7 constant_dynamic-update-slice_fusion.18
  52.0 1.9 %collective-permute-start.4 = (bf16[64,1664]{1,0:T(8,128)(2,1)S(1)}, bf16[64,1664]{1,0:T(8,128)(2,1)S(1)}, u32[]{:S(2)}, u32[]{:S(2)}) collective-permute-start(bf16[64,1664]{1,0:T(8,128)(2,1)S(1)} %collective-permute-done.2), channel_id=1, source_target_pairs={{0,64},{32,96},{64,128},{96,160},{128,192},{160,224},{192,256},{22... | collective-permute-start | bytes 638984 | tf_op jit(solution)/shard_map/ppermute | solution.py:87
  54.0 0.7 constant_dynamic-update-slice_fusion.17
  54.7 4.5 %collective-permute-start.5 = (bf16[64,1664]{1,0:T(8,128)(2,1)S(1)}, bf16[64,1664]{1,0:T(8,128)(2,1)S(1)}, u32[]{:S(2)}, u32[]{:S(2)}) collective-permute-start(bf16[64,1664]{1,0:T(8,128)(2,1)S(1)} %collective-permute-done.3), channel_id=1, source_target_pairs={{0,448},{32,480},{64,0},{96,32},{128,64},{160,96},{192,128},{224,1... | collective-permute-start | bytes 638984 | tf_op jit(solution)/shard_map/ppermute | solution.py:90
  59.9 1.9 %collective-permute-start.6 = (bf16[64,1664]{1,0:T(8,128)(2,1)S(1)}, bf16[64,1664]{1,0:T(8,128)(2,1)S(1)}, u32[]{:S(2)}, u32[]{:S(2)}) collective-permute-start(bf16[64,1664]{1,0:T(8,128)(2,1)S(1)} %collective-permute-done.4), channel_id=1, source_target_pairs={{0,64},{32,96},{64,128},{96,160},{128,192},{160,224},{192,256},{22... | collective-permute-start | bytes 638984 | tf_op jit(solution)/shard_map/ppermute | solution.py:87
  61.9 0.7 constant_dynamic-update-slice_fusion.15
  62.6 0.7 constant_dynamic-update-slice_fusion.14
  63.3 4.5 %collective-permute-done.6 = bf16[64,1664]{1,0:T(8,128)(2,1)S(1)} collective-permute-done((bf16[64,1664]{1,0:T(8,128)(2,1)S(1)}, bf16[64,1664]{1,0:T(8,128)(2,1)S(1)}, u32[]{:S(2)}, u32[]{:S(2)}) %collective-permute-start.6) | collective-permute-done | bytes 213024 | tf_op jit(solution)/shard_map/ppermute | solution.py:87
  68.4 8.9 %collective-permute-start.7 = (bf16[512,1664]{1,0:T(8,128)(2,1)}, bf16[512,1664]{1,0:T(8,128)(2,1)S(1)}, u32[]{:S(2)}, u32[]{:S(2)}) collective-permute-start(bf16[512,1664]{1,0:T(8,128)(2,1)} %bitcast.24), channel_id=1, source_target_pairs={{0,32},{32,0},{64,96},{96,64},{128,160},{160,128},{192,224},{224,1... | collective-permute-start | bytes 5111816 | tf_op jit(solution)/shard_map/ppermute | solution.py:97
  77.4 1.6 fusion.119
  85.1 2.1 %collective-permute-start.8 = (bf16[256,1792]{1,0:T(8,128)(2,1)S(1)}, bf16[256,1792]{1,0:T(8,128)(2,1)S(1)}, u32[]{:S(2)}, u32[]{:S(2)}) collective-permute-start(bf16[256,1792]{1,0:T(8,128)(2,1)S(1)} %pad_maximum_fusion), channel_id=1, source_target_pairs={{0,32},{32,0},{64,96},{96,64},{128,160},{160,128},{192,224},{224,1... | collective-permute-start | bytes 2752520 | tf_op jit(solution)/shard_map/ppermute | solution.py:152
  88.5 1.0 collective-permute-done.8
  89.5 1.2 fusion.10
  90.7 4.2 %all-to-all-start.1 = ((bf16[8,32,1792]{2,1,0:T(8,128)(2,1)}), bf16[8,32,1792]{2,1,0:T(8,128)(2,1)}, u32[]{:S(2)}, u32[]{:S(2)}) async-start(bf16[8,32,1792]{2,1,0:T(8,128)(2,1)} %bitcast.100), calls=%async_computation.1 | async-start | bytes 1835008 | tf_op jit(solution)/shard_map/all_to_all | solution.py:156
  95.0 26.4 %all-to-all-done.1 = bf16[8,32,1792]{2,1,0:T(8,128)(2,1)} async-done(((bf16[8,32,1792]{2,1,0:T(8,128)(2,1)}), bf16[8,32,1792]{2,1,0:T(8,128)(2,1)}, u32[]{:S(2)}, u32[]{:S(2)}) %all-to-all-start.1) | async-done | bytes 917536 | tf_op jit(solution)/shard_map/all_to_all | solution.py:156
  121.4 1.3 convert_reduce_fusion
  122.7 1.2 fusion.7
  123.9 1.9 %reshape.248 = bf16[32,4,1664]{2,1,0:T(4,128)(2,1)} reshape(bf16[128,1664]{1,0:T(8,128)(2,1)} %fusion.7) | data formatting | bytes 851968 | tf_op jit(solution)/shard_map/reshape | solution.py:176
  125.8 6.6 %all-to-all-start.2 = ((bf16[32,4,1664]{2,1,0:T(4,128)(2,1)}), bf16[32,4,1664]{2,1,0:T(4,128)(2,1)}, u32[]{:S(2)}, u32[]{:S(2)}) async-start(bf16[32,4,1664]{2,1,0:T(4,128)(2,1)} %reshape.248), calls=%async_computation.2 | async-start | bytes 851968 | tf_op jit(solution)/shard_map/all_to_all | solution.py:175
  132.3 1.6 fusion.27
  133.9 1.4 fusion.5
  135.3 1.6 fusion.23
  137.0 7.7 %all-to-all-done.2 = bf16[32,4,1664]{2,1,0:T(4,128)(2,1)} async-done(((bf16[32,4,1664]{2,1,0:T(4,128)(2,1)}), bf16[32,4,1664]{2,1,0:T(4,128)(2,1)}, u32[]{:S(2)}, u32[]{:S(2)}) %all-to-all-start.2) | async-done | bytes 426016 | tf_op jit(solution)/shard_map/all_to_all | solution.py:175
  144.7 1.9 %reshape.249 = bf16[128,1664]{1,0:T(8,128)(2,1)} reshape(bf16[32,4,1664]{2,1,0:T(4,128)(2,1)} %all-to-all-done.2) | data formatting | bytes 851968 | tf_op jit(solution)/shard_map/reshape | solution.py:181
  146.5 1.2 fusion.94
  147.8 0.8 broadcast_in_dim.88
  148.5 7.1 %all-to-all-start.3 = ((f32[16,2,1664]{2,1,0:T(2,128)}), f32[16,2,1664]{2,1,0:T(2,128)}, u32[]{:S(2)}, u32[]{:S(2)}) async-start(f32[16,2,1664]{2,1,0:T(2,128)} %broadcast_in_dim.88), calls=%async_computation.3 | async-start | bytes 425984 | tf_op jit(solution)/shard_map/all_to_all | solution.py:187
  155.7 2.3 %fusion.4 = bf16[1,256,1664]{2,1,0:T(8,128)(2,1)} fusion(f32[256,1664]{1,0:T(8,128)S(1)} %copy-done.3, bf16[256,1664]{1,0:T(8,128)(2,1)S(1)} %bitcast.99, f32[256]{0:T(256)S(1)} %get-tuple-element.8, f32[256,256]{0,1:T(8,128)} %copy-done.4), kind=kOutput, calls=%fused_computation.10 | convolution fusion | flops 219480064 | bytes 3671040 | tf_op jit(solution)/shard_map/dot_general | solution.py:11
  158.0 1.1 convolution_convert_fusion
  159.2 7.3 %all-to-all-done.3 = f32[16,2,1664]{2,1,0:T(2,128)} async-done(((f32[16,2,1664]{2,1,0:T(2,128)}), f32[16,2,1664]{2,1,0:T(2,128)}, u32[]{:S(2)}, u32[]{:S(2)}) %all-to-all-start.3) | async-done | bytes 213024 | tf_op jit(solution)/shard_map/all_to_all | solution.py:187
  166.4 1.1 reshape.250
  167.5 0.7 bitcast_bitcast_fusion
  (98 shorter events, 10.2 us)
Async XLA Ops:
  0.6 78.8 %copy-start = (bf16[1,1664,256]{2,1,0:T(8,128)(2,1)S(1)}, bf16[1,1664,256]{2,1,0:T(8,128)(2,1)}, u32[]{:S(2)}) copy-start(bf16[1,1664,256]{2,1,0:T(8,128)(2,1)} %param.12) | copy-start | bytes 2555908
  5.4 13.1 %copy-start.14 = (f32[1664,32]{0,1:T(8,128)S(1)}, f32[1664,32]{0,1:T(8,128)}, u32[]{:S(2)}) copy-start(f32[1664,32]{0,1:T(8,128)} %param.11) | copy-start | bytes 638980
  6.3 22.8 %all-to-all-start = ((bf16[32,4,1664]{2,1,0:T(4,128)(2,1)}), bf16[32,4,1664]{2,1,0:T(4,128)(2,1)S(1)}, u32[]{:S(2)}, u32[]{:S(2)}) async-start(bf16[32,4,1664]{2,1,0:T(4,128)(2,1)} %reshape.236), calls=%async_computation | async-start | bytes 851968 | tf_op jit(solution)/shard_map/all_to_all | solution.py:66
  29.5 14.7 %collective-permute-start = (bf16[64,1664]{1,0:T(8,128)(2,1)S(1)}, bf16[64,1664]{1,0:T(8,128)(2,1)S(1)}, u32[]{:S(2)}, u32[]{:S(2)}) collective-permute-start(bf16[64,1664]{1,0:T(8,128)(2,1)S(1)} %convolution_convert_fusion.1), channel_id=1, source_target_pairs={{0,64},{32,96},{64,128},{96,160},{128,192},{160,224},{192,256},{22... | collective-permute-start | bytes 638984 | tf_op jit(solution)/shard_map/ppermute | solution.py:87
  33.5 13.3 %collective-permute-start.1 = (bf16[64,1664]{1,0:T(8,128)(2,1)S(1)}, bf16[64,1664]{1,0:T(8,128)(2,1)S(1)}, u32[]{:S(2)}, u32[]{:S(2)}) collective-permute-start(bf16[64,1664]{1,0:T(8,128)(2,1)S(1)} %convolution_convert_fusion.1), channel_id=1, source_target_pairs={{0,448},{32,480},{64,0},{96,32},{128,64},{160,96},{192,128},{224,1... | collective-permute-start | bytes 638984 | tf_op jit(solution)/shard_map/ppermute | solution.py:90
  44.1 7.9 %collective-permute-start.2 = (bf16[64,1664]{1,0:T(8,128)(2,1)S(1)}, bf16[64,1664]{1,0:T(8,128)(2,1)S(1)}, u32[]{:S(2)}, u32[]{:S(2)}) collective-permute-start(bf16[64,1664]{1,0:T(8,128)(2,1)S(1)} %collective-permute-done), channel_id=1, source_target_pairs={{0,64},{32,96},{64,128},{96,160},{128,192},{160,224},{192,256},{22... | collective-permute-start | bytes 638984 | tf_op jit(solution)/shard_map/ppermute | solution.py:87
  46.7 8.0 %collective-permute-start.3 = (bf16[64,1664]{1,0:T(8,128)(2,1)S(1)}, bf16[64,1664]{1,0:T(8,128)(2,1)S(1)}, u32[]{:S(2)}, u32[]{:S(2)}) collective-permute-start(bf16[64,1664]{1,0:T(8,128)(2,1)S(1)} %collective-permute-done.1), channel_id=1, source_target_pairs={{0,448},{32,480},{64,0},{96,32},{128,64},{160,96},{192,128},{224,1... | collective-permute-start | bytes 638984 | tf_op jit(solution)/shard_map/ppermute | solution.py:90
  52.0 7.9 %collective-permute-start.4 = (bf16[64,1664]{1,0:T(8,128)(2,1)S(1)}, bf16[64,1664]{1,0:T(8,128)(2,1)S(1)}, u32[]{:S(2)}, u32[]{:S(2)}) collective-permute-start(bf16[64,1664]{1,0:T(8,128)(2,1)S(1)} %collective-permute-done.2), channel_id=1, source_target_pairs={{0,64},{32,96},{64,128},{96,160},{128,192},{160,224},{192,256},{22... | collective-permute-start | bytes 638984 | tf_op jit(solution)/shard_map/ppermute | solution.py:87
  54.7 7.9 %collective-permute-start.5 = (bf16[64,1664]{1,0:T(8,128)(2,1)S(1)}, bf16[64,1664]{1,0:T(8,128)(2,1)S(1)}, u32[]{:S(2)}, u32[]{:S(2)}) collective-permute-start(bf16[64,1664]{1,0:T(8,128)(2,1)S(1)} %collective-permute-done.3), channel_id=1, source_target_pairs={{0,448},{32,480},{64,0},{96,32},{128,64},{160,96},{192,128},{224,1... | collective-permute-start | bytes 638984 | tf_op jit(solution)/shard_map/ppermute | solution.py:90
  59.9 7.8 %collective-permute-start.6 = (bf16[64,1664]{1,0:T(8,128)(2,1)S(1)}, bf16[64,1664]{1,0:T(8,128)(2,1)S(1)}, u32[]{:S(2)}, u32[]{:S(2)}) collective-permute-start(bf16[64,1664]{1,0:T(8,128)(2,1)S(1)} %collective-permute-done.4), channel_id=1, source_target_pairs={{0,64},{32,96},{64,128},{96,160},{128,192},{160,224},{192,256},{22... | collective-permute-start | bytes 638984 | tf_op jit(solution)/shard_map/ppermute | solution.py:87
  68.4 12.5 %collective-permute-start.7 = (bf16[512,1664]{1,0:T(8,128)(2,1)}, bf16[512,1664]{1,0:T(8,128)(2,1)S(1)}, u32[]{:S(2)}, u32[]{:S(2)}) collective-permute-start(bf16[512,1664]{1,0:T(8,128)(2,1)} %bitcast.24), channel_id=1, source_target_pairs={{0,32},{32,0},{64,96},{96,64},{128,160},{160,128},{192,224},{224,1... | collective-permute-start | bytes 5111816 | tf_op jit(solution)/shard_map/ppermute | solution.py:97
  77.4 1.6 copy-start.12
  77.4 1.6 copy-start.15
  79.0 1.0 copy-start.1
  79.0 1.5 copy-start.13
  80.0 7.6 %copy-start.4 = (f32[256,256]{0,1:T(8,128)}, f32[256,256]{0,1:T(8,128)S(1)}, u32[]{:S(2)}) copy-start(f32[256,256]{0,1:T(8,128)S(1)} %fusion.17) | copy-start | bytes 786436
  80.9 6.6 %copy-start.9 = (f32[256,256]{0,1:T(8,128)}, f32[256,256]{0,1:T(8,128)S(1)}, u32[]{:S(2)}) copy-start(f32[256,256]{0,1:T(8,128)S(1)} %get-tuple-element.35) | copy-start | bytes 786436
  82.0 1.0 copy-start.6
  82.4 0.9 copy-start.11
  85.1 4.4 %collective-permute-start.8 = (bf16[256,1792]{1,0:T(8,128)(2,1)S(1)}, bf16[256,1792]{1,0:T(8,128)(2,1)S(1)}, u32[]{:S(2)}, u32[]{:S(2)}) collective-permute-start(bf16[256,1792]{1,0:T(8,128)(2,1)S(1)} %pad_maximum_fusion), channel_id=1, source_target_pairs={{0,32},{32,0},{64,96},{96,64},{128,160},{160,128},{192,224},{224,1... | collective-permute-start | bytes 2752520 | tf_op jit(solution)/shard_map/ppermute | solution.py:152
  90.7 30.7 %all-to-all-start.1 = ((bf16[8,32,1792]{2,1,0:T(8,128)(2,1)}), bf16[8,32,1792]{2,1,0:T(8,128)(2,1)}, u32[]{:S(2)}, u32[]{:S(2)}) async-start(bf16[8,32,1792]{2,1,0:T(8,128)(2,1)} %bitcast.100), calls=%async_computation.1 | async-start | bytes 1835008 | tf_op jit(solution)/shard_map/all_to_all | solution.py:156
  125.8 18.9 %all-to-all-start.2 = ((bf16[32,4,1664]{2,1,0:T(4,128)(2,1)}), bf16[32,4,1664]{2,1,0:T(4,128)(2,1)}, u32[]{:S(2)}, u32[]{:S(2)}) async-start(bf16[32,4,1664]{2,1,0:T(4,128)(2,1)} %reshape.248), calls=%async_computation.2 | async-start | bytes 851968 | tf_op jit(solution)/shard_map/all_to_all | solution.py:175
  132.3 1.6 copy-start.5
  132.3 1.6 copy-start.10
  133.9 1.4 copy-start.7
  135.3 20.3 %copy-start.2 = (bf16[1,8,32,1664]{3,2,1,0:T(8,128)(2,1)S(1)}, bf16[1,8,32,1664]{3,2,1,0:T(8,128)(2,1)}, u32[]{:S(2)}) copy-start(bf16[1,8,32,1664]{3,2,1,0:T(8,128)(2,1)} %copy-done.1) | copy-start | bytes 2555908
  137.0 18.7 %copy-start.3 = (f32[256,1664]{1,0:T(8,128)S(1)}, f32[256,1664]{1,0:T(8,128)}, u32[]{:S(2)}) copy-start(f32[256,1664]{1,0:T(8,128)} %fusion.23) | copy-start | bytes 5111812
  148.5 17.9 %all-to-all-start.3 = ((f32[16,2,1664]{2,1,0:T(2,128)}), f32[16,2,1664]{2,1,0:T(2,128)}, u32[]{:S(2)}, u32[]{:S(2)}) async-start(f32[16,2,1664]{2,1,0:T(2,128)} %broadcast_in_dim.88), calls=%async_computation.3 | async-start | bytes 425984 | tf_op jit(solution)/shard_map/all_to_all | solution.py:187
  155.7 2.3 %copy-start.8 = (bf16[128,1664]{1,0:T(8,128)(2,1)S(1)}, bf16[128,1664]{1,0:T(8,128)(2,1)}, u32[]{:S(2)}) copy-start(bf16[128,1664]{1,0:T(8,128)(2,1)} %reshape.249) | copy-start | bytes 1277956
where the time goes:
time: 170 us; the launch traced here: 168 us
  starting transfers between devices  66.9 us (39%)
  waiting for transfers between devices  56.7 us (33%)
  matrix products  19.5 us (11%)
  local copies, waits for them, and re-layouts  16.9 us (10%)
  other arithmetic  6.87 us (4%)
    all_to_all x1, waiting for transfers between devices, grads(): lax.all_to_all(own_rows.astype(jnp.bfloat16).reshape(chips, cap, width +...  26.4 us
    ppermute x3, starting transfers between devices, grads(): lax.ppermute(down, 'dp', [(i, (i - 2) % groups) for i in range(groups)])  17.7 us
    all_to_all x1, starting transfers between devices, grads(): lax.all_to_all(send, 'expert', split_axis=0, concat_axis=0, tiled=True)  10.5 us
    dot_general x10, matrix products, dot_rows(): lax.dot_general(left, right, (((0,), (0,)), ((), ())), preferred_element_...  10.3 us
    all_to_all x1, waiting for transfers between devices, grads(): lax.all_to_all(send, 'expert', split_axis=0, concat_axis=0, tiled=True)  9.83 us
    ppermute x4, starting transfers between devices, grads(): up = lax.ppermute(up, 'dp', [(i, (i + 2) % groups) for i in range(groups)])  9.73 us
    ppermute x1, starting transfers between devices, grads(): other = lax.ppermute(own, 'dp', swap)  8.93 us
    all_to_all x1, waiting for transfers between devices, grads(): lax.all_to_all(back_rows.astype(jnp.bfloat16).reshape(experts, 2 * SLOT,...  7.7 us
  transfers between devices with their start and end apart: 13, of which 6 were waited for; matrix products, arithmetic and copies ran while one was open for 12% of the time, Pallas kernels for 0%

commit v1 on v0

--- a/solution.py
+++ b/solution.py
@@ -77,7 +77,8 @@
     chips = groups // 2
     here = lax.axis_index("dp") // 2
     shape = (chips, cap, width)
-    blocks = jnp.zeros((2,) + shape, jnp.bfloat16)
+    blocks_x = jnp.zeros(shape, jnp.bfloat16)
+    blocks_dy = jnp.zeros(shape, jnp.bfloat16)
     up = down = slab
     for step in range(chips // 2 + 1):
         arrived = []
@@ -90,13 +91,13 @@
                 down = lax.ppermute(down, "dp", [(i, (i - 2) % groups) for i in range(groups)])
                 arrived.append((down, (here + step) % chips))
         for block, spot in arrived:
-            block = block.reshape(2, 1, cap, width)
-            blocks = lax.dynamic_update_slice(blocks, block, (0, spot, 0, 0))
+            blocks_x = lax.dynamic_update_slice(blocks_x, block[None, :cap], (spot, 0, 0))
+            blocks_dy = lax.dynamic_update_slice(blocks_dy, block[None, cap:], (spot, 0, 0))
     swap = [(i, i ^ 1) for i in range(groups)]
-    own = blocks.reshape(2 * chips * cap, width)
-    other = lax.ppermute(own, "dp", swap)
-    own_x, own_dy = own[: chips * cap], own[chips * cap :]
-    other_x, other_dy = other[: chips * cap], other[chips * cap :]
+    own_x = blocks_x.reshape(chips * cap, width)
+    own_dy = blocks_dy.reshape(chips * cap, width)
+    other_x = lax.ppermute(own_x, "dp", swap)
+    other_dy = lax.ppermute(own_dy, "dp", swap)
 
     router_parts = split_bf16(router, 3)
     router_wide = jnp.concatenate(router_parts, axis=1)
@@ -142,7 +143,8 @@
     row_id = jnp.arange(chips * cap, dtype=jnp.int32)
 
     def dealt(side):
-        unit = (2 * (row_id // cap) + side) * deal + row_id % cap
+        group, spot = 2 * (row_id // cap) + side, row_id % cap
+        unit = spot % tiles * experts + SLOT * group + spot // tiles
         pick = one_hot(jnp.where(row_id % cap < deal, unit, -1), experts * tiles)
         return dot_plain(pick, router_part)
 
@@ -153,23 +155,25 @@
     own_rows = row_grads(own_pre, own_hi, own_lo, own_extra)
     own_rows = own_rows + partner_rows.astype(jnp.float32)
     columns = [[i for i in range(groups) if i % 2 == side] for side in range(2)]
+    own_rows = own_rows.astype(jnp.bfloat16).reshape(chips, cap, width + 128)
     pieces = lax.all_to_all(
-        own_rows.astype(jnp.bfloat16).reshape(chips, cap, width + 128),
+        own_rows,
         "dp",
         split_axis=0,
         concat_axis=0,
         axis_index_groups=columns,
         tiled=True,
     )
-    pieces = jnp.sum(pieces.astype(jnp.float32), axis=0)
-    row_sum = pieces[:, :width].astype(jnp.bfloat16)
-    router_rows = pieces[:deal, width:].reshape(SLOT, width)
-
-    grad_in = (dot_rows(own_x, own_pre) + dot_rows(other_x, other_pre)).astype(jnp.bfloat16)
-    grad_out = (dot_rows(own_gated, own_dy) + dot_rows(other_gated, other_dy)).astype(jnp.bfloat16)
+    router_rows = jnp.sum(pieces[:, :deal, width:].astype(jnp.float32), axis=0)
+    router_rows = router_rows.reshape(SLOT, width)
+
+    grad_in = dot_rows(own_x, own_pre) + dot_rows(other_x, other_pre)
+    grad_out = dot_rows(own_gated, own_dy) + dot_rows(other_gated, other_dy)
+    grad_in, grad_out = grad_in.astype(jnp.bfloat16), grad_out.astype(jnp.bfloat16)
 
     slot = lax.broadcasted_iota(jnp.int32, (experts * 2 * SLOT, 1), 0) % (2 * SLOT)
-    back_rows = dot_rows(one_hot(place_x, experts * 2 * SLOT), row_sum)
+    spread = one_hot(jnp.tile(place_x, chips), experts * 2 * SLOT)
+    back_rows = dot_rows(spread, pieces[:, :, :width].reshape(chips * cap, width))
     for part in range(SLOT):
         back_rows += jnp.where(slot == SLOT + part, router_rows[part : part + 1], 0.0)
     ret = lax.all_to_all(
@@ -178,15 +182,12 @@
         split_axis=0,
         concat_axis=0,
         tiled=True,
-    ).reshape(experts * 2 * SLOT, width)
-    grad_tokens = dot_rows(pick_x, ret).astype(jnp.bfloat16)
-    spot = lax.broadcasted_iota(jnp.int32, (SLOT, experts * 2 * SLOT), 1)
-    line = lax.broadcasted_iota(jnp.int32, (SLOT, experts * 2 * SLOT), 0)
-    router_rows = dot_plain((spot % (2 * SLOT) == SLOT + line).astype(jnp.bfloat16), ret)
+    )
+    router_rows = jnp.sum(ret[:, SLOT:].astype(jnp.float32), axis=0)
+    grad_tokens = dot_rows(pick_x, ret.reshape(experts * 2 * SLOT, width)).astype(jnp.bfloat16)
     router_rows = jnp.broadcast_to(router_rows[None], (groups, SLOT, width))
     router_rows = lax.all_to_all(router_rows, "dp", split_axis=0, concat_axis=0, tiled=True)
-    router_rows = router_rows.reshape(tiles, experts, 128)
-    grad_router = jnp.swapaxes(router_rows, 0, 1).reshape(experts, width).T
+    grad_router = router_rows.reshape(experts, width).T
     return grad_tokens, grad_in[None], grad_out[None], grad_router
 
 

time: 170 us -> 173 us (1.018)
  waiting for transfers between devices: 56.7 us -> 67.1 us
  local copies, waits for them, and re-layouts: 16.9 us -> 9.02 us
  starting transfers between devices: 66.9 us -> 69.6 us
  matrix products: 19.5 us -> 17 us
    ppermute x4, waiting for transfers between devices: 4.47 us -> 12.7 us  [grads(): up = lax.ppermute(up, 'dp', [(i, (i + 2) % groups) for i in range(groups)])]
    dynamic_update_slice x8 -> x9, local copies, waits for them, and re-layouts: 5.63 us -> 0.24 us  [the longest x8 0.22 us: grads(): lax.dynamic_update_slice(blocks_x, block[None, :cap], (spot, 0, 0))]
    ppermute x1 -> x2, starting transfers between devices: 8.93 us -> 12.3 us  [the longest x1 10.3 us: grads(): other_dy = lax.ppermute(own_dy, 'dp', swap)]
    ppermute x3, starting transfers between devices: 17.7 us -> 20.7 us  [grads(): lax.ppermute(down, 'dp', [(i, (i - 2) % groups) for i in range(groups)])]
    ppermute x4, starting transfers between devices: 9.73 us -> 7.66 us  [grads(): up = lax.ppermute(up, 'dp', [(i, (i + 2) % groups) for i in range(groups)])]
    dot_general x10 -> x9, matrix products: 6.43 us -> 5.2 us  [dot_plain(): return jnp.dot(left, right, preferred_element_type=jnp.float32)]
  transfers between devices with their start and end apart: 13 -> 14, of which waited for: 6 -> 10; matrix products, arithmetic and copies ran while one was open for 12% -> 8% of each run, Pallas kernels for 0% -> 0%
where the time goes in v1:
time: 173 us; the launch traced here: 172 us
  starting transfers between devices  69.6 us (40%)
  waiting for transfers between devices  67.1 us (39%)
  matrix products  17 us (10%)
  local copies, waits for them, and re-layouts  9.02 us (5%)
  other arithmetic  7.72 us (4%)
    all_to_all x1, waiting for transfers between devices, grads(): lax.all_to_all(own_rows, 'dp', split_axis=0, concat_axis=0, axis_index_gr...  26.3 us
    ppermute x3, starting transfers between devices, grads(): lax.ppermute(down, 'dp', [(i, (i - 2) % groups) for i in range(groups)])  20.7 us
    ppermute x4, waiting for transfers between devices, grads(): up = lax.ppermute(up, 'dp', [(i, (i + 2) % groups) for i in range(groups)])  12.7 us
    all_to_all x1, starting transfers between devices, grads(): lax.all_to_all(send, 'expert', split_axis=0, concat_axis=0, tiled=True)  10.5 us
    ppermute x1, starting transfers between devices, grads(): other_dy = lax.ppermute(own_dy, 'dp', swap)  10.3 us
    all_to_all x1, waiting for transfers between devices, grads(): lax.all_to_all(send, 'expert', split_axis=0, concat_axis=0, tiled=True)  9.84 us
    dot_general x10, matrix products, dot_rows(): lax.dot_general(left, right, (((0,), (0,)), ((), ())), preferred_element_...  9.02 us
    all_to_all x1, waiting for transfers between devices, grads(): lax.all_to_all(back_rows.astype(jnp.bfloat16).reshape(experts, 2 * SLOT,...  8.9 us
  transfers between devices with their start and end apart: 14, of which 10 were waited for; matrix products, arithmetic and copies ran while one was open for 8% of the time, Pallas kernels for 0%

profile of v1, /device:TPU:1, one launch (start us, length us, event | category | flops | bytes accessed | tf_op | source)
XLA Modules:
  0.0 171.9 jit_solution(1054167548544169827)
XLA Ops:
  0.7 0.7 maximum_convert_fusion
  1.4 0.9 fusion.98
  2.7 1.3 fusion.75
  4.0 1.4 fusion.6
  5.4 0.9 reshape.229
  6.3 10.5 %all-to-all-start = ((bf16[32,4,1664]{2,1,0:T(4,128)(2,1)}), bf16[32,4,1664]{2,1,0:T(4,128)(2,1)S(1)}, u32[]{:S(2)}, u32[]{:S(2)}) async-start(bf16[32,4,1664]{2,1,0:T(4,128)(2,1)} %reshape.229), calls=%async_computation | async-start | bytes 851968 | tf_op jit(solution)/shard_map/all_to_all | solution.py:66
  16.8 0.7 and_select_fusion.7
  17.7 0.8 broadcast_add_fusion
  18.5 0.7 reduce-precision_convert_fusion
  19.3 9.8 %all-to-all-done = bf16[32,4,1664]{2,1,0:T(4,128)(2,1)S(1)} async-done(((bf16[32,4,1664]{2,1,0:T(4,128)(2,1)}), bf16[32,4,1664]{2,1,0:T(4,128)(2,1)S(1)}, u32[]{:S(2)}, u32[]{:S(2)}) %all-to-all-start) | async-done | bytes 426016 | tf_op jit(solution)/shard_map/all_to_all | solution.py:66
  29.5 10.7 %collective-permute-start.1 = (bf16[64,1664]{1,0:T(8,128)(2,1)S(1)}, bf16[64,1664]{1,0:T(8,128)(2,1)S(1)}, u32[]{:S(2)}, u32[]{:S(2)}) collective-permute-start(bf16[64,1664]{1,0:T(8,128)(2,1)S(1)} %convolution_convert_fusion.1), channel_id=1, source_target_pairs={{0,448},{32,480},{64,0},{96,32},{128,64},{160,96},{192,128},{224,1... | collective-permute-start | bytes 638984 | tf_op jit(solution)/shard_map/ppermute | solution.py:91
  40.1 1.9 %collective-permute-start = (bf16[64,1664]{1,0:T(8,128)(2,1)S(1)}, bf16[64,1664]{1,0:T(8,128)(2,1)S(1)}, u32[]{:S(2)}, u32[]{:S(2)}) collective-permute-start(bf16[64,1664]{1,0:T(8,128)(2,1)S(1)} %convolution_convert_fusion.1), channel_id=1, source_target_pairs={{0,64},{32,96},{64,128},{96,160},{128,192},{160,224},{192,256},{22... | collective-permute-start | bytes 638984 | tf_op jit(solution)/shard_map/ppermute | solution.py:88
  42.3 0.6 collective-permute-done.1
  42.9 5.0 %collective-permute-start.3 = (bf16[64,1664]{1,0:T(8,128)(2,1)S(1)}, bf16[64,1664]{1,0:T(8,128)(2,1)S(1)}, u32[]{:S(2)}, u32[]{:S(2)}) collective-permute-start(bf16[64,1664]{1,0:T(8,128)(2,1)S(1)} %collective-permute-done.1), channel_id=1, source_target_pairs={{0,448},{32,480},{64,0},{96,32},{128,64},{160,96},{192,128},{224,1... | collective-permute-start | bytes 638984 | tf_op jit(solution)/shard_map/ppermute | solution.py:91
  47.9 1.9 %collective-permute-start.2 = (bf16[64,1664]{1,0:T(8,128)(2,1)S(1)}, bf16[64,1664]{1,0:T(8,128)(2,1)S(1)}, u32[]{:S(2)}, u32[]{:S(2)}) collective-permute-start(bf16[64,1664]{1,0:T(8,128)(2,1)S(1)} %collective-permute-done), channel_id=1, source_target_pairs={{0,64},{32,96},{64,128},{96,160},{128,192},{160,224},{192,256},{22... | collective-permute-start | bytes 638984 | tf_op jit(solution)/shard_map/ppermute | solution.py:88
  49.9 0.8 collective-permute-done.3
  50.7 5.0 %collective-permute-start.5 = (bf16[64,1664]{1,0:T(8,128)(2,1)S(1)}, bf16[64,1664]{1,0:T(8,128)(2,1)S(1)}, u32[]{:S(2)}, u32[]{:S(2)}) collective-permute-start(bf16[64,1664]{1,0:T(8,128)(2,1)S(1)} %collective-permute-done.3), channel_id=1, source_target_pairs={{0,448},{32,480},{64,0},{96,32},{128,64},{160,96},{192,128},{224,1... | collective-permute-start | bytes 638984 | tf_op jit(solution)/shard_map/ppermute | solution.py:91
  55.7 1.9 %collective-permute-start.4 = (bf16[64,1664]{1,0:T(8,128)(2,1)S(1)}, bf16[64,1664]{1,0:T(8,128)(2,1)S(1)}, u32[]{:S(2)}, u32[]{:S(2)}) collective-permute-start(bf16[64,1664]{1,0:T(8,128)(2,1)S(1)} %collective-permute-done.2), channel_id=1, source_target_pairs={{0,64},{32,96},{64,128},{96,160},{128,192},{160,224},{192,256},{22... | collective-permute-start | bytes 638984 | tf_op jit(solution)/shard_map/ppermute | solution.py:88
  57.7 5.8 %collective-permute-done.4 = bf16[64,1664]{1,0:T(8,128)(2,1)S(1)} collective-permute-done((bf16[64,1664]{1,0:T(8,128)(2,1)S(1)}, bf16[64,1664]{1,0:T(8,128)(2,1)S(1)}, u32[]{:S(2)}, u32[]{:S(2)}) %collective-permute-start.4) | collective-permute-done | bytes 213024 | tf_op jit(solution)/shard_map/ppermute | solution.py:88
  63.5 1.9 %collective-permute-start.6 = (bf16[64,1664]{1,0:T(8,128)(2,1)S(1)}, bf16[64,1664]{1,0:T(8,128)(2,1)S(1)}, u32[]{:S(2)}, u32[]{:S(2)}) collective-permute-start(bf16[64,1664]{1,0:T(8,128)(2,1)S(1)} %collective-permute-done.4), channel_id=1, source_target_pairs={{0,64},{32,96},{64,128},{96,160},{128,192},{160,224},{192,256},{22... | collective-permute-start | bytes 638984 | tf_op jit(solution)/shard_map/ppermute | solution.py:88
  65.5 6.9 %collective-permute-done.6 = bf16[64,1664]{1,0:T(8,128)(2,1)S(1)} collective-permute-done((bf16[64,1664]{1,0:T(8,128)(2,1)S(1)}, bf16[64,1664]{1,0:T(8,128)(2,1)S(1)}, u32[]{:S(2)}, u32[]{:S(2)}) %collective-permute-start.6) | collective-permute-done | bytes 213024 | tf_op jit(solution)/shard_map/ppermute | solution.py:88
  72.4 10.3 %collective-permute-start.8 = (bf16[256,1664]{1,0:T(8,128)(2,1)S(1)}, bf16[256,1664]{1,0:T(8,128)(2,1)S(1)}, u32[]{:S(2)}, u32[]{:S(2)}) collective-permute-start(bf16[256,1664]{1,0:T(8,128)(2,1)S(1)} %bitcast.139), channel_id=1, source_target_pairs={{0,32},{32,0},{64,96},{96,64},{128,160},{160,128},{192,224},{224,1... | collective-permute-start | bytes 2555912 | tf_op jit(solution)/shard_map/ppermute | solution.py:100
  82.8 1.9 %collective-permute-start.7 = (bf16[256,1664]{1,0:T(8,128)(2,1)S(1)}, bf16[256,1664]{1,0:T(8,128)(2,1)S(1)}, u32[]{:S(2)}, u32[]{:S(2)}) collective-permute-start(bf16[256,1664]{1,0:T(8,128)(2,1)S(1)} %bitcast.133), channel_id=1, source_target_pairs={{0,32},{32,0},{64,96},{96,64},{128,160},{160,128},{192,224},{224,1... | collective-permute-start | bytes 2555912 | tf_op jit(solution)/shard_map/ppermute | solution.py:99
  85.2 0.5 fusion.17
  86.3 0.7 collective-permute-done.7
  90.0 0.5 fusion.11
  91.3 2.0 %collective-permute-start.9 = (bf16[256,1792]{1,0:T(8,128)(2,1)S(1)}, bf16[256,1792]{1,0:T(8,128)(2,1)S(1)}, u32[]{:S(2)}, u32[]{:S(2)}) collective-permute-start(bf16[256,1792]{1,0:T(8,128)(2,1)S(1)} %pad_maximum_fusion), channel_id=1, source_target_pairs={{0,32},{32,0},{64,96},{96,64},{128,160},{160,128},{192,224},{224,1... | collective-permute-start | bytes 2752520 | tf_op jit(solution)/shard_map/ppermute | solution.py:154
  93.7 0.5 fusion.15
  94.7 1.0 collective-permute-done.9
  95.7 1.2 fusion.10
  96.9 4.2 %all-to-all-start.1 = ((bf16[8,32,1792]{2,1,0:T(8,128)(2,1)}), bf16[8,32,1792]{2,1,0:T(8,128)(2,1)}, u32[]{:S(2)}, u32[]{:S(2)}) async-start(bf16[8,32,1792]{2,1,0:T(8,128)(2,1)} %bitcast.142), calls=%async_computation.1 | async-start | bytes 1835008 | tf_op jit(solution)/shard_map/all_to_all | solution.py:159
  101.2 26.3 %all-to-all-done.1 = bf16[8,32,1792]{2,1,0:T(8,128)(2,1)} async-done(((bf16[8,32,1792]{2,1,0:T(8,128)(2,1)}), bf16[8,32,1792]{2,1,0:T(8,128)(2,1)}, u32[]{:S(2)}, u32[]{:S(2)}) %all-to-all-start.1) | async-done | bytes 917536 | tf_op jit(solution)/shard_map/all_to_all | solution.py:159
  127.6 0.9 convert_reduce_fusion.1
  128.4 1.2 slice.205
  129.6 1.2 fusion.7
  130.8 1.9 %reshape.235 = bf16[32,4,1664]{2,1,0:T(4,128)(2,1)} reshape(bf16[128,1664]{1,0:T(8,128)(2,1)} %fusion.7) | data formatting | bytes 851968 | tf_op jit(solution)/shard_map/reshape | solution.py:180
  132.7 5.1 %all-to-all-start.2 = ((bf16[32,4,1664]{2,1,0:T(4,128)(2,1)}), bf16[32,4,1664]{2,1,0:T(4,128)(2,1)}, u32[]{:S(2)}, u32[]{:S(2)}) async-start(bf16[32,4,1664]{2,1,0:T(4,128)(2,1)} %reshape.235), calls=%async_computation.2 | async-start | bytes 851968 | tf_op jit(solution)/shard_map/all_to_all | solution.py:179
  137.9 1.6 fusion.112
  139.5 1.4 fusion.5
  141.3 8.9 %all-to-all-done.2 = bf16[32,4,1664]{2,1,0:T(4,128)(2,1)} async-done(((bf16[32,4,1664]{2,1,0:T(4,128)(2,1)}), bf16[32,4,1664]{2,1,0:T(4,128)(2,1)}, u32[]{:S(2)}, u32[]{:S(2)}) %all-to-all-start.2) | async-done | bytes 426016 | tf_op jit(solution)/shard_map/all_to_all | solution.py:179
  150.2 1.3 convert_reduce_fusion
  151.5 0.7 broadcast_in_dim.147
  152.2 7.1 %all-to-all-start.3 = ((f32[16,2,1664]{2,1,0:T(2,128)}), f32[16,2,1664]{2,1,0:T(2,128)}, u32[]{:S(2)}, u32[]{:S(2)}) async-start(f32[16,2,1664]{2,1,0:T(2,128)} %broadcast_in_dim.147), calls=%async_computation.3 | async-start | bytes 425984 | tf_op jit(solution)/shard_map/all_to_all | solution.py:189
  159.4 2.3 %fusion.4 = bf16[1,256,1664]{2,1,0:T(8,128)(2,1)} fusion(f32[256,1664]{1,0:T(8,128)S(1)} %fusion.49, bf16[256,1664]{1,0:T(8,128)(2,1)S(1)} %bitcast.141, f32[256]{0:T(256)S(1)} %get-tuple-element.8, f32[256,256]{0,1:T(8,128)} %copy-done.1), kind=kOutput, calls=%fused_computation.10 | convolution fusion | flops 219480064 | bytes 3671040 | tf_op jit(solution)/shard_map/dot_general | solution.py:11
  161.6 1.1 reshape.236
  162.8 1.1 convolution_convert_fusion
  163.9 6.2 %all-to-all-done.3 = f32[16,2,1664]{2,1,0:T(2,128)} async-done(((f32[16,2,1664]{2,1,0:T(2,128)}), f32[16,2,1664]{2,1,0:T(2,128)}, u32[]{:S(2)}, u32[]{:S(2)}) %all-to-all-start.3) | async-done | bytes 213024 | tf_op jit(solution)/shard_map/all_to_all | solution.py:189
  170.1 1.8 %reshape.237 = f32[32,1664]{1,0:T(8,128)} reshape(f32[16,2,1664]{2,1,0:T(2,128)} %all-to-all-done.3) | data formatting | bytes 425984 | tf_op jit(solution)/shard_map/reshape | solution.py:190
  (96 shorter events, 7.3 us)
Async XLA Ops:
  0.6 84.5 %copy-start = (bf16[1,1664,256]{2,1,0:T(8,128)(2,1)S(1)}, bf16[1,1664,256]{2,1,0:T(8,128)(2,1)}, u32[]{:S(2)}) copy-start(bf16[1,1664,256]{2,1,0:T(8,128)(2,1)} %param.12) | copy-start | bytes 2555908
  5.4 13.1 %copy-start.12 = (f32[1664,32]{0,1:T(8,128)S(1)}, f32[1664,32]{0,1:T(8,128)}, u32[]{:S(2)}) copy-start(f32[1664,32]{0,1:T(8,128)} %param.11) | copy-start | bytes 638980
  6.3 22.8 %all-to-all-start = ((bf16[32,4,1664]{2,1,0:T(4,128)(2,1)}), bf16[32,4,1664]{2,1,0:T(4,128)(2,1)S(1)}, u32[]{:S(2)}, u32[]{:S(2)}) async-start(bf16[32,4,1664]{2,1,0:T(4,128)(2,1)} %reshape.229), calls=%async_computation | async-start | bytes 851968 | tf_op jit(solution)/shard_map/all_to_all | solution.py:66
  29.5 13.4 %collective-permute-start.1 = (bf16[64,1664]{1,0:T(8,128)(2,1)S(1)}, bf16[64,1664]{1,0:T(8,128)(2,1)S(1)}, u32[]{:S(2)}, u32[]{:S(2)}) collective-permute-start(bf16[64,1664]{1,0:T(8,128)(2,1)S(1)} %convolution_convert_fusion.1), channel_id=1, source_target_pairs={{0,448},{32,480},{64,0},{96,32},{128,64},{160,96},{192,128},{224,1... | collective-permute-start | bytes 638984 | tf_op jit(solution)/shard_map/ppermute | solution.py:91
  40.1 7.8 %collective-permute-start = (bf16[64,1664]{1,0:T(8,128)(2,1)S(1)}, bf16[64,1664]{1,0:T(8,128)(2,1)S(1)}, u32[]{:S(2)}, u32[]{:S(2)}) collective-permute-start(bf16[64,1664]{1,0:T(8,128)(2,1)S(1)} %convolution_convert_fusion.1), channel_id=1, source_target_pairs={{0,64},{32,96},{64,128},{96,160},{128,192},{160,224},{192,256},{22... | collective-permute-start | bytes 638984 | tf_op jit(solution)/shard_map/ppermute | solution.py:88
  42.2 42.5 %copy-start.11 = (bf16[1664,32]{0,1:T(8,128)(2,1)S(1)}, bf16[1664,32]{0,1:T(8,128)(2,1)}, u32[]{:S(2)}) copy-start(bf16[1664,32]{0,1:T(8,128)(2,1)} %get-tuple-element.17) | copy-start | bytes 319492
  42.2 42.5 %copy-start.13 = (bf16[1664,32]{0,1:T(8,128)(2,1)S(1)}, bf16[1664,32]{0,1:T(8,128)(2,1)}, u32[]{:S(2)}) copy-start(bf16[1664,32]{0,1:T(8,128)(2,1)} %get-tuple-element.16) | copy-start | bytes 319492
  42.9 7.8 %collective-permute-start.3 = (bf16[64,1664]{1,0:T(8,128)(2,1)S(1)}, bf16[64,1664]{1,0:T(8,128)(2,1)S(1)}, u32[]{:S(2)}, u32[]{:S(2)}) collective-permute-start(bf16[64,1664]{1,0:T(8,128)(2,1)S(1)} %collective-permute-done.1), channel_id=1, source_target_pairs={{0,448},{32,480},{64,0},{96,32},{128,64},{160,96},{192,128},{224,1... | collective-permute-start | bytes 638984 | tf_op jit(solution)/shard_map/ppermute | solution.py:91
  47.9 7.8 %collective-permute-start.2 = (bf16[64,1664]{1,0:T(8,128)(2,1)S(1)}, bf16[64,1664]{1,0:T(8,128)(2,1)S(1)}, u32[]{:S(2)}, u32[]{:S(2)}) collective-permute-start(bf16[64,1664]{1,0:T(8,128)(2,1)S(1)} %collective-permute-done), channel_id=1, source_target_pairs={{0,64},{32,96},{64,128},{96,160},{128,192},{160,224},{192,256},{22... | collective-permute-start | bytes 638984 | tf_op jit(solution)/shard_map/ppermute | solution.py:88
  50.7 14.8 %collective-permute-start.5 = (bf16[64,1664]{1,0:T(8,128)(2,1)S(1)}, bf16[64,1664]{1,0:T(8,128)(2,1)S(1)}, u32[]{:S(2)}, u32[]{:S(2)}) collective-permute-start(bf16[64,1664]{1,0:T(8,128)(2,1)S(1)} %collective-permute-done.3), channel_id=1, source_target_pairs={{0,448},{32,480},{64,0},{96,32},{128,64},{160,96},{192,128},{224,1... | collective-permute-start | bytes 638984 | tf_op jit(solution)/shard_map/ppermute | solution.py:91
  55.7 7.8 %collective-permute-start.4 = (bf16[64,1664]{1,0:T(8,128)(2,1)S(1)}, bf16[64,1664]{1,0:T(8,128)(2,1)S(1)}, u32[]{:S(2)}, u32[]{:S(2)}) collective-permute-start(bf16[64,1664]{1,0:T(8,128)(2,1)S(1)} %collective-permute-done.2), channel_id=1, source_target_pairs={{0,64},{32,96},{64,128},{96,160},{128,192},{160,224},{192,256},{22... | collective-permute-start | bytes 638984 | tf_op jit(solution)/shard_map/ppermute | solution.py:88
  63.5 8.9 %collective-permute-start.6 = (bf16[64,1664]{1,0:T(8,128)(2,1)S(1)}, bf16[64,1664]{1,0:T(8,128)(2,1)S(1)}, u32[]{:S(2)}, u32[]{:S(2)}) collective-permute-start(bf16[64,1664]{1,0:T(8,128)(2,1)S(1)} %collective-permute-done.4), channel_id=1, source_target_pairs={{0,64},{32,96},{64,128},{96,160},{128,192},{160,224},{192,256},{22... | collective-permute-start | bytes 638984 | tf_op jit(solution)/shard_map/ppermute | solution.py:88
  72.4 15.7 %collective-permute-start.8 = (bf16[256,1664]{1,0:T(8,128)(2,1)S(1)}, bf16[256,1664]{1,0:T(8,128)(2,1)S(1)}, u32[]{:S(2)}, u32[]{:S(2)}) collective-permute-start(bf16[256,1664]{1,0:T(8,128)(2,1)S(1)} %bitcast.139), channel_id=1, source_target_pairs={{0,32},{32,0},{64,96},{96,64},{128,160},{160,128},{192,224},{224,1... | collective-permute-start | bytes 2555912 | tf_op jit(solution)/shard_map/ppermute | solution.py:100
  82.8 4.3 %collective-permute-start.7 = (bf16[256,1664]{1,0:T(8,128)(2,1)S(1)}, bf16[256,1664]{1,0:T(8,128)(2,1)S(1)}, u32[]{:S(2)}, u32[]{:S(2)}) collective-permute-start(bf16[256,1664]{1,0:T(8,128)(2,1)S(1)} %bitcast.133), channel_id=1, source_target_pairs={{0,32},{32,0},{64,96},{96,64},{128,160},{160,128},{192,224},{224,1... | collective-permute-start | bytes 2555912 | tf_op jit(solution)/shard_map/ppermute | solution.py:99
  84.7 1.2 copy-start.5
  85.9 7.8 %copy-start.1 = (f32[256,256]{0,1:T(8,128)}, f32[256,256]{0,1:T(8,128)S(1)}, u32[]{:S(2)}) copy-start(f32[256,256]{0,1:T(8,128)S(1)} %fusion.17) | copy-start | bytes 786436
  86.3 7.4 %copy-start.8 = (f32[256,256]{0,1:T(8,128)}, f32[256,256]{0,1:T(8,128)S(1)}, u32[]{:S(2)}) copy-start(f32[256,256]{0,1:T(8,128)S(1)} %get-tuple-element.47) | copy-start | bytes 786436
  88.1 1.9 %copy-start.3 = (f32[256,256]{0,1:T(8,128)}, f32[256,256]{0,1:T(8,128)S(1)}, u32[]{:S(2)}) copy-start(f32[256,256]{0,1:T(8,128)S(1)} %fusion.13) | copy-start | bytes 786436
  88.1 0.9 copy-start.6
  88.6 1.4 copy-start.10
  91.3 4.4 %collective-permute-start.9 = (bf16[256,1792]{1,0:T(8,128)(2,1)S(1)}, bf16[256,1792]{1,0:T(8,128)(2,1)S(1)}, u32[]{:S(2)}, u32[]{:S(2)}) collective-permute-start(bf16[256,1792]{1,0:T(8,128)(2,1)S(1)} %pad_maximum_fusion), channel_id=1, source_target_pairs={{0,32},{32,0},{64,96},{96,64},{128,160},{160,128},{192,224},{224,1... | collective-permute-start | bytes 2752520 | tf_op jit(solution)/shard_map/ppermute | solution.py:154
  96.9 30.6 %all-to-all-start.1 = ((bf16[8,32,1792]{2,1,0:T(8,128)(2,1)}), bf16[8,32,1792]{2,1,0:T(8,128)(2,1)}, u32[]{:S(2)}, u32[]{:S(2)}) async-start(bf16[8,32,1792]{2,1,0:T(8,128)(2,1)} %bitcast.142), calls=%async_computation.1 | async-start | bytes 1835008 | tf_op jit(solution)/shard_map/all_to_all | solution.py:159
  132.7 17.5 %all-to-all-start.2 = ((bf16[32,4,1664]{2,1,0:T(4,128)(2,1)}), bf16[32,4,1664]{2,1,0:T(4,128)(2,1)}, u32[]{:S(2)}, u32[]{:S(2)}) async-start(bf16[32,4,1664]{2,1,0:T(4,128)(2,1)} %reshape.235), calls=%async_computation.2 | async-start | bytes 851968 | tf_op jit(solution)/shard_map/all_to_all | solution.py:179
  137.8 1.6 copy-start.2
  137.8 1.6 copy-start.9
  139.4 1.4 copy-start.4
  139.4 1.4 copy-start.7
  152.2 17.9 %all-to-all-start.3 = ((f32[16,2,1664]{2,1,0:T(2,128)}), f32[16,2,1664]{2,1,0:T(2,128)}, u32[]{:S(2)}, u32[]{:S(2)}) async-start(f32[16,2,1664]{2,1,0:T(2,128)} %broadcast_in_dim.147), calls=%async_computation.3 | async-start | bytes 425984 | tf_op jit(solution)/shard_map/all_to_all | solution.py:189

commit v2 on v1

--- a/solution.py
+++ b/solution.py
@@ -74,90 +74,90 @@
     place_x = owner * (2 * SLOT) + rank
     pack = one_hot(jnp.concatenate([place_x, place_x + SLOT]), experts * 2 * SLOT)
     slab = dot_plain(pack, recv).astype(jnp.bfloat16)
+    swap = [(i, i ^ 1) for i in range(groups)]
+    partner_in = lax.ppermute(block_in, "dp", swap)
+    partner_out = lax.ppermute(block_out, "dp", swap)
+
     chips = groups // 2
     here = lax.axis_index("dp") // 2
     shape = (chips, cap, width)
     blocks_x = jnp.zeros(shape, jnp.bfloat16)
     blocks_dy = jnp.zeros(shape, jnp.bfloat16)
-    up = down = slab
+    core = lax.axis_index("dp") % 2
+    toward = 2 * core - 1
+    first_hop = [(i, (i + 2 - 4 * (i % 2)) % groups) for i in range(groups)]
+    second_hop = [(i, (i - 2 + 4 * (i % 2)) % groups) for i in range(groups)]
+    first = second = slab
     for step in range(chips // 2 + 1):
         arrived = []
         if step == 0:
             arrived.append((slab, here))
         else:
-            up = lax.ppermute(up, "dp", [(i, (i + 2) % groups) for i in range(groups)])
-            arrived.append((up, (here - step) % chips))
+            first = lax.ppermute(first, "dp", first_hop)
+            arrived.append((first, (here + toward * step) % chips))
             if step < chips // 2:
-                down = lax.ppermute(down, "dp", [(i, (i - 2) % groups) for i in range(groups)])
-                arrived.append((down, (here + step) % chips))
+                second = lax.ppermute(second, "dp", second_hop)
+                arrived.append((second, (here - toward * step) % chips))
         for block, spot in arrived:
             blocks_x = lax.dynamic_update_slice(blocks_x, block[None, :cap], (spot, 0, 0))
             blocks_dy = lax.dynamic_update_slice(blocks_dy, block[None, cap:], (spot, 0, 0))
-    swap = [(i, i ^ 1) for i in range(groups)]
-    own_x = blocks_x.reshape(chips * cap, width)
-    own_dy = blocks_dy.reshape(chips * cap, width)
-    other_x = lax.ppermute(own_x, "dp", swap)
-    other_dy = lax.ppermute(own_dy, "dp", swap)
+    rows_x = blocks_x.reshape(chips * cap, width)
+    rows_dy = blocks_dy.reshape(chips * cap, width)
 
     router_parts = split_bf16(router, 3)
     router_wide = jnp.concatenate(router_parts, axis=1)
     router_back = jnp.concatenate([router_parts[0], router_parts[0], router_parts[1]], axis=1)
     mark = (lax.broadcasted_iota(jnp.int32, (1, experts), 1) == me).astype(jnp.float32)
 
-    def hidden_grads(rows_x, rows_dy):
-        logit_parts = dot_plain(rows_x, router_wide)
-        logits = (
-            logit_parts[:, 2 * experts :] + logit_parts[:, experts : 2 * experts]
-        ) + logit_parts[:, :experts]
-        prob = jax.nn.softmax(logits, axis=-1)
-        gate = jnp.sum(prob * mark, axis=-1, keepdims=True)
-        pre = dot_plain(rows_x, block_in)
+    logit_parts = dot_plain(rows_x, router_wide)
+    logits = (
+        logit_parts[:, 2 * experts :] + logit_parts[:, experts : 2 * experts]
+    ) + logit_parts[:, :experts]
+    prob = jax.nn.softmax(logits, axis=-1)
+    gate = jnp.sum(prob * mark, axis=-1, keepdims=True)
+
+    def hidden_grads(mat_in, mat_out):
+        pre = dot_plain(rows_x, mat_in)
         cdf = 0.5 * (1.0 + lax.erf(pre * 0.7071067811865476))
         slope = cdf + pre * jnp.exp(-0.5 * pre * pre) * 0.3989422804014327
         act = (pre * cdf).astype(jnp.bfloat16)
-        dy_hidden = dot_cols(rows_dy, block_out)
+        dy_hidden = dot_cols(rows_dy, mat_out)
         gate_part = jnp.sum(act.astype(jnp.float32) * dy_hidden, axis=-1, keepdims=True)
         pre_grad = (gate * dy_hidden * slope).astype(jnp.bfloat16)
         gated = (gate * act.astype(jnp.float32)).astype(jnp.bfloat16)
-        return pre_grad, gated, (gate_part * gate) * (mark - prob)
+        return pre_grad, gated, gate_part
+
+    own_pre, own_gated, own_gate = hidden_grads(block_in, block_out)
+    other_pre, other_gated, other_gate = hidden_grads(partner_in, partner_out)
+    gate_part = own_gate + other_gate
+
+    share_hi, share_lo = split_bf16((gate_part * gate) * (mark - prob), 2)
 
     tiles = width // 128
     deal = experts * tiles // groups
-
-    def row_grads(pre_grad, share_hi, share_lo, extra):
-        left = jnp.concatenate([share_hi, share_lo, share_hi], axis=1)
-        rows = dot_cols(pre_grad, block_in) + dot_cols(left, router_back)
-        return jnp.concatenate([rows, extra], axis=1)
-
-    other_pre, other_gated, other_share = hidden_grads(other_x, other_dy)
-    own_pre, own_gated, own_share = hidden_grads(own_x, own_dy)
-    own_hi, own_lo = split_bf16(own_share, 2)
-    other_hi, other_lo = split_bf16(other_share, 2)
-    router_part = dot_rows(own_hi, own_x) + dot_rows(own_lo, own_x)
-    router_part += dot_rows(other_hi, other_x) + dot_rows(other_lo, other_x)
+    row_id = jnp.arange(chips * cap, dtype=jnp.int32)
+    router_part = dot_rows(share_hi, rows_x) + dot_rows(share_lo, rows_x)
     router_part = router_part.astype(jnp.bfloat16)
     router_part = jnp.concatenate(
         [router_part[:, 128 * tile : 128 * (tile + 1)] for tile in range(tiles)]
     )
-    core = lax.axis_index("dp") % 2
-    row_id = jnp.arange(chips * cap, dtype=jnp.int32)
 
     def dealt(side):
         group, spot = 2 * (row_id // cap) + side, row_id % cap
         unit = spot % tiles * experts + SLOT * group + spot // tiles
-        pick = one_hot(jnp.where(row_id % cap < deal, unit, -1), experts * tiles)
+        pick = one_hot(jnp.where(spot < deal, unit, -1), experts * tiles)
         return dot_plain(pick, router_part)
 
-    own_extra, other_extra = dealt(core), dealt(1 - core)
-
-    other_rows = row_grads(other_pre, other_hi, other_lo, other_extra)
-    partner_rows = lax.ppermute(other_rows.astype(jnp.bfloat16), "dp", swap)
-    own_rows = row_grads(own_pre, own_hi, own_lo, own_extra)
-    own_rows = own_rows + partner_rows.astype(jnp.float32)
+    partner_extra = lax.ppermute(dealt(1 - core).astype(jnp.bfloat16), "dp", swap)
+    extra = (dealt(core) + partner_extra.astype(jnp.float32)).astype(jnp.bfloat16)
+
+    left = jnp.concatenate([share_hi, share_lo, share_hi], axis=1)
+    rows = dot_cols(own_pre, block_in) + dot_cols(other_pre, partner_in)
+    rows = (rows + dot_cols(left, router_back)).astype(jnp.bfloat16)
+    rows = jnp.concatenate([rows, extra], axis=1).reshape(chips, cap, width + 128)
     columns = [[i for i in range(groups) if i % 2 == side] for side in range(2)]
-    own_rows = own_rows.astype(jnp.bfloat16).reshape(chips, cap, width + 128)
     pieces = lax.all_to_all(
-        own_rows,
+        rows,
         "dp",
         split_axis=0,
         concat_axis=0,
@@ -167,8 +167,12 @@
     router_rows = jnp.sum(pieces[:, :deal, width:].astype(jnp.float32), axis=0)
     router_rows = router_rows.reshape(SLOT, width)
 
-    grad_in = dot_rows(own_x, own_pre) + dot_rows(other_x, other_pre)
-    grad_out = dot_rows(own_gated, own_dy) + dot_rows(other_gated, other_dy)
+    trade_in = dot_rows(rows_x, other_pre).astype(jnp.bfloat16)
+    trade_out = dot_rows(other_gated, rows_dy).astype(jnp.bfloat16)
+    trade_in = lax.ppermute(trade_in, "dp", swap)
+    trade_out = lax.ppermute(trade_out, "dp", swap)
+    grad_in = dot_rows(rows_x, own_pre) + trade_in.astype(jnp.float32)
+    grad_out = dot_rows(own_gated, rows_dy) + trade_out.astype(jnp.float32)
     grad_in, grad_out = grad_in.astype(jnp.bfloat16), grad_out.astype(jnp.bfloat16)
 
     slot = lax.broadcasted_iota(jnp.int32, (experts * 2 * SLOT, 1), 0) % (2 * SLOT)
@@ -185,9 +189,10 @@
     )
     router_rows = jnp.sum(ret[:, SLOT:].astype(jnp.float32), axis=0)
     grad_tokens = dot_rows(pick_x, ret.reshape(experts * 2 * SLOT, width)).astype(jnp.bfloat16)
+    router_rows = router_rows.astype(jnp.bfloat16)
     router_rows = jnp.broadcast_to(router_rows[None], (groups, SLOT, width))
     router_rows = lax.all_to_all(router_rows, "dp", split_axis=0, concat_axis=0, tiled=True)
-    grad_router = router_rows.reshape(experts, width).T
+    grad_router = router_rows.reshape(experts, width).astype(jnp.float32).T
     return grad_tokens, grad_in[None], grad_out[None], grad_router
 
 

time: 173 us -> 161 us (0.931)
  waiting for transfers between devices: 67.1 us -> 48.3 us
  starting transfers between devices: 69.6 us -> 77.5 us
  matrix products: 17 us -> 20.9 us
  local copies, waits for them, and re-layouts: 9.02 us -> 5.55 us
    ppermute x10 -> x12, starting transfers between devices: 42.7 us -> 51 us  [the longest x4 25.2 us: grads(): first = lax.ppermute(first, 'dp', first_hop)]
    all_to_all x1, waiting for transfers between devices: 26.3 us -> 19.3 us  [grads(): lax.all_to_all(rows, 'dp', split_axis=0, concat_axis=0, axis_index_groups...]
    ppermute x10 -> x12, waiting for transfers between devices: 15.9 us -> 9.2 us  [the longest x3 7.13 us: grads(): second = lax.ppermute(second, 'dp', second_hop)]
    all_to_all x1, waiting for transfers between devices: 9.84 us -> 5.04 us  [grads(): lax.all_to_all(send, 'expert', split_axis=0, concat_axis=0, tiled=True)]
    dot_general x6 -> x5, matrix products: 2.81 us -> 5.99 us  [dot_cols(): lax.dot_general(left, right, (((1,), (1,)), ((), ())), preferred_element_...]
    reshape x1 -> x0, local copies, waits for them, and re-layouts: 1.76 us -> none  [grads(): grad_router = router_rows.reshape(experts, width).T]
    dot_general x10 -> x8, matrix products: 9.02 us -> 9.84 us  [dot_rows(): lax.dot_general(left, right, (((0,), (0,)), ((), ())), preferred_element_...]
    dot_general x9 -> x8, matrix products: 5.2 us -> 5.04 us  [dot_plain(): return jnp.dot(left, right, preferred_element_type=jnp.float32)]
  transfers between devices with their start and end apart: 14 -> 16, of which waited for: 10 -> 9; matrix products, arithmetic and copies ran while one was open for 8% -> 14% of each run, Pallas kernels for 0% -> 0%
where the time goes in v2:
time: 161 us; the launch traced here: 160 us
  starting transfers between devices  77.5 us (48%)
  waiting for transfers between devices  48.3 us (30%)
  matrix products  20.9 us (13%)
  other arithmetic  6.36 us (4%)
  local copies, waits for them, and re-layouts  5.55 us (3%)
    ppermute x4, starting transfers between devices, grads(): first = lax.ppermute(first, 'dp', first_hop)  25.2 us
    all_to_all x1, waiting for transfers between devices, grads(): lax.all_to_all(rows, 'dp', split_axis=0, concat_axis=0, axis_index_groups...  19.3 us
    ppermute x1, starting transfers between devices, grads(): lax.ppermute(dealt(1 - core).astype(jnp.bfloat16), 'dp', swap)  11 us
    all_to_all x1, starting transfers between devices, grads(): lax.all_to_all(send, 'expert', split_axis=0, concat_axis=0, tiled=True)  10.5 us
    dot_general x8, matrix products, dot_rows(): lax.dot_general(left, right, (((0,), (0,)), ((), ())), preferred_element_...  9.84 us
    all_to_all x1, waiting for transfers between devices, grads(): lax.all_to_all(router_rows, 'dp', split_axis=0, concat_axis=0, tiled=True)  7.42 us
    all_to_all x1, waiting for transfers between devices, grads(): lax.all_to_all(back_rows.astype(jnp.bfloat16).reshape(experts, 2 * SLOT,...  7.32 us
    ppermute x3, waiting for transfers between devices, grads(): second = lax.ppermute(second, 'dp', second_hop)  7.13 us
  transfers between devices with their start and end apart: 16, of which 9 were waited for; matrix products, arithmetic and copies ran while one was open for 14% of the time, Pallas kernels for 0%

profile of v2, /device:TPU:1, one launch (start us, length us, event | category | flops | bytes accessed | tf_op | source)
XLA Modules:
  0.0 159.9 jit_solution(12561064110587511539)
XLA Ops:
  0.7 0.9 fusion.75
  1.8 0.7 maximum_convert_fusion
  3.0 1.4 fusion.6
  4.5 0.9 reshape.224
  5.3 10.5 %all-to-all-start = ((bf16[32,4,1664]{2,1,0:T(4,128)(2,1)}), bf16[32,4,1664]{2,1,0:T(4,128)(2,1)S(1)}, u32[]{:S(2)}, u32[]{:S(2)}) async-start(bf16[32,4,1664]{2,1,0:T(4,128)(2,1)} %reshape.224), calls=%async_computation | async-start | bytes 851968 | tf_op jit(solution)/shard_map/all_to_all | solution.py:66
  15.8 2.9 %collective-permute-start.8 = (bf16[1664,256]{1,0:T(8,128)(2,1)S(1)}, bf16[1664,256]{1,0:T(8,128)(2,1)}, u32[]{:S(2)}, u32[]{:S(2)}) collective-permute-start(bf16[1664,256]{1,0:T(8,128)(2,1)S(1)} %bitcast.135), channel_id=1, source_target_pairs={{0,32},{32,0},{64,96},{96,64},{128,160},{160,128},{192,224},{224,1... | collective-permute-start | bytes 2555912 | tf_op jit(solution)/shard_map/ppermute | solution.py:78
  18.7 1.9 %collective-permute-start.7 = (bf16[256,1664]{1,0:T(8,128)(2,1)}, bf16[256,1664]{1,0:T(8,128)(2,1)}, u32[]{:S(2)}, u32[]{:S(2)}) collective-permute-start(bf16[256,1664]{1,0:T(8,128)(2,1)} %bitcast.22), channel_id=1, source_target_pairs={{0,32},{32,0},{64,96},{96,64},{128,160},{160,128},{192,224},{224,1... | collective-permute-start | bytes 2555912 | tf_op jit(solution)/shard_map/ppermute | solution.py:79
  20.6 0.7 and_select_fusion.7
  21.4 0.8 broadcast_add_fusion
  22.4 0.7 reduce-precision_convert_fusion
  23.1 5.0 %all-to-all-done = bf16[32,4,1664]{2,1,0:T(4,128)(2,1)S(1)} async-done(((bf16[32,4,1664]{2,1,0:T(4,128)(2,1)}), bf16[32,4,1664]{2,1,0:T(4,128)(2,1)S(1)}, u32[]{:S(2)}, u32[]{:S(2)}) %all-to-all-start) | async-done | bytes 426016 | tf_op jit(solution)/shard_map/all_to_all | solution.py:66
  28.5 10.7 %collective-permute-start = (bf16[64,1664]{1,0:T(8,128)(2,1)S(1)}, bf16[64,1664]{1,0:T(8,128)(2,1)S(1)}, u32[]{:S(2)}, u32[]{:S(2)}) collective-permute-start(bf16[64,1664]{1,0:T(8,128)(2,1)S(1)} %convolution_convert_fusion.3), channel_id=1, source_target_pairs={{0,64},{32,480},{64,128},{96,32},{128,192},{160,96},{192,256},{224... | collective-permute-start | bytes 638984 | tf_op jit(solution)/shard_map/ppermute | solution.py:96
  39.2 1.9 %collective-permute-start.1 = (bf16[64,1664]{1,0:T(8,128)(2,1)S(1)}, bf16[64,1664]{1,0:T(8,128)(2,1)S(1)}, u32[]{:S(2)}, u32[]{:S(2)}) collective-permute-start(bf16[64,1664]{1,0:T(8,128)(2,1)S(1)} %convolution_convert_fusion.3), channel_id=1, source_target_pairs={{0,448},{32,96},{64,0},{96,160},{128,64},{160,224},{192,128},{224,... | collective-permute-start | bytes 638984 | tf_op jit(solution)/shard_map/ppermute | solution.py:99
  41.3 0.6 collective-permute-done
  42.0 5.0 %collective-permute-start.2 = (bf16[64,1664]{1,0:T(8,128)(2,1)S(1)}, bf16[64,1664]{1,0:T(8,128)(2,1)S(1)}, u32[]{:S(2)}, u32[]{:S(2)}) collective-permute-start(bf16[64,1664]{1,0:T(8,128)(2,1)S(1)} %collective-permute-done), channel_id=1, source_target_pairs={{0,64},{32,480},{64,128},{96,32},{128,192},{160,96},{192,256},{224... | collective-permute-start | bytes 638984 | tf_op jit(solution)/shard_map/ppermute | solution.py:96
  47.0 1.5 collective-permute-done.1
  48.4 1.9 %collective-permute-start.3 = (bf16[64,1664]{1,0:T(8,128)(2,1)S(1)}, bf16[64,1664]{1,0:T(8,128)(2,1)S(1)}, u32[]{:S(2)}, u32[]{:S(2)}) collective-permute-start(bf16[64,1664]{1,0:T(8,128)(2,1)S(1)} %collective-permute-done.1), channel_id=1, source_target_pairs={{0,448},{32,96},{64,0},{96,160},{128,64},{160,224},{192,128},{224,... | collective-permute-start | bytes 638984 | tf_op jit(solution)/shard_map/ppermute | solution.py:99
  50.4 4.8 %collective-permute-start.4 = (bf16[64,1664]{1,0:T(8,128)(2,1)S(1)}, bf16[64,1664]{1,0:T(8,128)(2,1)S(1)}, u32[]{:S(2)}, u32[]{:S(2)}) collective-permute-start(bf16[64,1664]{1,0:T(8,128)(2,1)S(1)} %collective-permute-done.2), channel_id=1, source_target_pairs={{0,64},{32,480},{64,128},{96,32},{128,192},{160,96},{192,256},{224... | collective-permute-start | bytes 638984 | tf_op jit(solution)/shard_map/ppermute | solution.py:96
  55.2 3.3 %collective-permute-done.3 = bf16[64,1664]{1,0:T(8,128)(2,1)S(1)} collective-permute-done((bf16[64,1664]{1,0:T(8,128)(2,1)S(1)}, bf16[64,1664]{1,0:T(8,128)(2,1)S(1)}, u32[]{:S(2)}, u32[]{:S(2)}) %collective-permute-start.3) | collective-permute-done | bytes 213024 | tf_op jit(solution)/shard_map/ppermute | solution.py:99
  58.5 1.9 %collective-permute-start.5 = (bf16[64,1664]{1,0:T(8,128)(2,1)S(1)}, bf16[64,1664]{1,0:T(8,128)(2,1)S(1)}, u32[]{:S(2)}, u32[]{:S(2)}) collective-permute-start(bf16[64,1664]{1,0:T(8,128)(2,1)S(1)} %collective-permute-done.3), channel_id=1, source_target_pairs={{0,448},{32,96},{64,0},{96,160},{128,64},{160,224},{192,128},{224,... | collective-permute-start | bytes 638984 | tf_op jit(solution)/shard_map/ppermute | solution.py:99
  60.5 4.8 %collective-permute-start.6 = (bf16[64,1664]{1,0:T(8,128)(2,1)S(1)}, bf16[64,1664]{1,0:T(8,128)(2,1)S(1)}, u32[]{:S(2)}, u32[]{:S(2)}) collective-permute-start(bf16[64,1664]{1,0:T(8,128)(2,1)S(1)} %collective-permute-done.4), channel_id=1, source_target_pairs={{0,64},{32,480},{64,128},{96,32},{128,192},{160,96},{192,256},{224... | collective-permute-start | bytes 638984 | tf_op jit(solution)/shard_map/ppermute | solution.py:96
  65.3 2.4 %collective-permute-done.5 = bf16[64,1664]{1,0:T(8,128)(2,1)S(1)} collective-permute-done((bf16[64,1664]{1,0:T(8,128)(2,1)S(1)}, bf16[64,1664]{1,0:T(8,128)(2,1)S(1)}, u32[]{:S(2)}, u32[]{:S(2)}) %collective-permute-start.5) | collective-permute-done | bytes 213024 | tf_op jit(solution)/shard_map/ppermute | solution.py:99
  67.7 1.4 collective-permute-done.6
  70.2 1.6 %fusion.99 = f32[256,256]{0,1:T(8,128)S(1)} fusion(bf16[256,1664]{1,0:T(8,128)(2,1)S(1)} %bitcast.125, bf16[1664,256]{1,0:T(8,128)(2,1)} %collective-permute-done.8), kind=kOutput, calls=%fused_computation.200 | convolution fusion | flops 218103808 | bytes 1966080 | tf_op jit(solution)/shard_map/dot_general | solution.py:23
  71.8 1.6 %fusion.20 = (f32[256]{0:T(256)S(1)}, f32[256,256]{0,1:T(8,128)S(1)}) fusion(f32[256,256]{0,1:T(8,128)S(1)} %fusion.89, bf16[256,1664]{1,0:T(8,128)(2,1)S(1)} %bitcast.130, bf16[1,256,1664]{2,1,0:T(8,128)(2,1)} %param.13), kind=kOutput, calls=%fused_computation.46 | convolution fusion | flops 218627840 | bytes 2229248 | tf_op jit(solution)/shard_map/dot_general | solution.py:17
  73.5 1.7 %fusion.22 = (f32[256]{0:T(256)S(1)}, f32[256,256]{0,1:T(8,128)S(1)}) fusion(f32[256,256]{0,1:T(8,128)S(1)} %fusion.99, bf16[256,1664]{1,0:T(8,128)(2,1)S(1)} %bitcast.131, bf16[256,1664]{1,0:T(8,128)(2,1)} %collective-permute-done.7), kind=kOutput, calls=%fused_computation.48 | convolution fusion | flops 218627840 | bytes 2229248 | tf_op jit(solution)/shard_map/dot_general | solution.py:17
  76.3 11.0 %collective-permute-start.9 = (bf16[256,128]{1,0:T(8,128)(2,1)S(1)}, bf16[256,128]{1,0:T(8,128)(2,1)S(1)}, u32[]{:S(2)}, u32[]{:S(2)}) collective-permute-start(bf16[256,128]{1,0:T(8,128)(2,1)S(1)} %convolution_convert_fusion.4), channel_id=1, source_target_pairs={{0,32},{32,0},{64,96},{96,64},{128,160},{160,128},{192,224},{224,1... | collective-permute-start | bytes 196616 | tf_op jit(solution)/shard_map/ppermute | solution.py:151
  87.2 0.5 fusion.87
  87.8 1.7 %convolution_add_fusion.3 = f32[256,1664]{1,0:T(8,128)S(1)} fusion(f32[256,1664]{1,0:T(8,128)S(1)} %fusion.87, bf16[1664,256]{1,0:T(8,128)(2,1)} %collective-permute-done.8, f32[256,256]{0,1:T(8,128)S(1)} %fusion.99, f32[256,256]{0,1:T(8,128)S(1)} %get-tuple-element.39, f32[256]{0:T(256)S(1)} %multiply_reduce_fusion), kind=kOutput, calls=%fused_computation.3 | convolution fusion | flops 219250688 | bytes 4785152 | tf_op jit(solution)/shard_map/dot_general | solution.py:17
  90.3 1.0 pad_maximum_fusion
  91.3 4.2 %all-to-all-start.1 = ((bf16[8,32,1792]{2,1,0:T(8,128)(2,1)}), bf16[8,32,1792]{2,1,0:T(8,128)(2,1)}, u32[]{:S(2)}, u32[]{:S(2)}) async-start(bf16[8,32,1792]{2,1,0:T(8,128)(2,1)} %bitcast.134), calls=%async_computation.1 | async-start | bytes 1835008 | tf_op jit(solution)/shard_map/all_to_all | solution.py:159
  95.6 1.4 convolution_convert_fusion.1
  97.0 1.9 %collective-permute-start.10 = (bf16[1664,256]{1,0:T(8,128)(2,1)}, bf16[1664,256]{1,0:T(8,128)(2,1)}, u32[]{:S(2)}, u32[]{:S(2)}) collective-permute-start(bf16[1664,256]{1,0:T(8,128)(2,1)} %convolution_convert_fusion.1), channel_id=1, source_target_pairs={{0,32},{32,0},{64,96},{96,64},{128,160},{160,128},{192,224},{224,1... | collective-permute-start | bytes 2555912 | tf_op jit(solution)/shard_map/ppermute | solution.py:172
  99.0 1.3 convolution_convert_fusion
  100.3 2.4 %collective-permute-start.11 = (bf16[256,1664]{1,0:T(8,128)(2,1)}, bf16[256,1664]{1,0:T(8,128)(2,1)}, u32[]{:S(2)}, u32[]{:S(2)}) collective-permute-start(bf16[256,1664]{1,0:T(8,128)(2,1)} %convolution_convert_fusion), channel_id=1, source_target_pairs={{0,32},{32,0},{64,96},{96,64},{128,160},{160,128},{192,224},{224,1... | collective-permute-start | bytes 2555912 | tf_op jit(solution)/shard_map/ppermute | solution.py:173
  102.7 19.3 %all-to-all-done.1 = bf16[8,32,1792]{2,1,0:T(8,128)(2,1)} async-done(((bf16[8,32,1792]{2,1,0:T(8,128)(2,1)}), bf16[8,32,1792]{2,1,0:T(8,128)(2,1)}, u32[]{:S(2)}, u32[]{:S(2)}) %all-to-all-start.1) | async-done | bytes 917536 | tf_op jit(solution)/shard_map/all_to_all | solution.py:159
  122.0 0.9 convert_reduce_fusion
  122.9 1.2 slice.190
  124.5 0.9 reshape.230
  125.4 5.2 %all-to-all-start.2 = ((bf16[32,4,1664]{2,1,0:T(4,128)(2,1)}), bf16[32,4,1664]{2,1,0:T(4,128)(2,1)S(1)}, u32[]{:S(2)}, u32[]{:S(2)}) async-start(bf16[32,4,1664]{2,1,0:T(4,128)(2,1)} %reshape.230), calls=%async_computation.2 | async-start | bytes 851968 | tf_op jit(solution)/shard_map/all_to_all | solution.py:183
  130.6 2.5 %fusion.4 = bf16[1,256,1664]{2,1,0:T(8,128)(2,1)} fusion(bf16[256,1664]{1,0:T(8,128)(2,1)S(1)} %bitcast.133, bf16[256,1664]{1,0:T(8,128)(2,1)} %collective-permute-done.11, f32[256]{0:T(256)S(1)} %multiply_reduce_fusion, f32[256,256]{0,1:T(8,128)S(1)} %fusion.89), kind=kOutput, calls=%fused_computation.12 | convolution fusion | flops 219906048 | bytes 2819072 | tf_op jit(solution)/shard_map/dot_general | solution.py:11
  133.1 2.5 %fusion.5 = bf16[1,1664,256]{2,1,0:T(8,128)(2,1)} fusion(bf16[256,1664]{1,0:T(8,128)(2,1)S(1)} %bitcast.129, bf16[1664,256]{1,0:T(8,128)(2,1)} %collective-permute-done.10, f32[256,256]{0,1:T(8,128)S(1)} %fusion.89, f32[256,256]{0,1:T(8,128)S(1)} %copy-done.3, f32[256]{0:T(256)S(1)} %multiply_reduce_fusion), kind=kOutput, calls=%fused_computation.13 | convolution fusion | flops 220102656 | bytes 3081216 | tf_op jit(solution)/shard_map/dot_general | solution.py:11
  135.7 7.3 %all-to-all-done.2 = bf16[32,4,1664]{2,1,0:T(4,128)(2,1)S(1)} async-done(((bf16[32,4,1664]{2,1,0:T(4,128)(2,1)}), bf16[32,4,1664]{2,1,0:T(4,128)(2,1)S(1)}, u32[]{:S(2)}, u32[]{:S(2)}) %all-to-all-start.2) | async-done | bytes 426016 | tf_op jit(solution)/shard_map/all_to_all | solution.py:183
  143.3 0.7 broadcast_in_dim.144
  144.0 6.5 %all-to-all-start.3 = ((bf16[16,2,1664]{2,1,0:T(2,128)(2,1)}), bf16[16,2,1664]{2,1,0:T(2,128)(2,1)S(1)}, u32[]{:S(2)}, u32[]{:S(2)}) async-start(bf16[16,2,1664]{2,1,0:T(2,128)(2,1)} %broadcast_in_dim.144), calls=%async_computation.3 | async-start | bytes 212992 | tf_op jit(solution)/shard_map/all_to_all | solution.py:194
  150.6 1.1 convolution_convert_fusion.2
  151.8 7.4 %all-to-all-done.3 = bf16[16,2,1664]{2,1,0:T(2,128)(2,1)S(1)} async-done(((bf16[16,2,1664]{2,1,0:T(2,128)(2,1)}), bf16[16,2,1664]{2,1,0:T(2,128)(2,1)S(1)}, u32[]{:S(2)}, u32[]{:S(2)}) %all-to-all-start.3) | async-done | bytes 106528 | tf_op jit(solution)/shard_map/all_to_all | solution.py:194
  159.2 0.7 reshape.232
  (89 shorter events, 5.3 us)
Async XLA Ops:
  0.6 2.0 %copy-start = (bf16[128,1664]{1,0:T(8,128)(2,1)S(1)}, bf16[128,1664]{1,0:T(8,128)(2,1)}, u32[]{:S(2)}) copy-start(bf16[128,1664]{1,0:T(8,128)(2,1)} %param.7) | copy-start | bytes 1277956
  3.0 12.8 %copy-start.1 = (bf16[1,1664,256]{2,1,0:T(8,128)(2,1)S(1)}, bf16[1,1664,256]{2,1,0:T(8,128)(2,1)}, u32[]{:S(2)}) copy-start(bf16[1,1664,256]{2,1,0:T(8,128)(2,1)} %param.12) | copy-start | bytes 2555908
  4.5 18.0 %copy-start.10 = (f32[1664,32]{0,1:T(8,128)S(1)}, f32[1664,32]{0,1:T(8,128)}, u32[]{:S(2)}) copy-start(f32[1664,32]{0,1:T(8,128)} %param.11) | copy-start | bytes 638980
  5.3 22.8 %all-to-all-start = ((bf16[32,4,1664]{2,1,0:T(4,128)(2,1)}), bf16[32,4,1664]{2,1,0:T(4,128)(2,1)S(1)}, u32[]{:S(2)}, u32[]{:S(2)}) async-start(bf16[32,4,1664]{2,1,0:T(4,128)(2,1)} %reshape.224), calls=%async_computation | async-start | bytes 851968 | tf_op jit(solution)/shard_map/all_to_all | solution.py:66
  15.8 54.4 %collective-permute-start.8 = (bf16[1664,256]{1,0:T(8,128)(2,1)S(1)}, bf16[1664,256]{1,0:T(8,128)(2,1)}, u32[]{:S(2)}, u32[]{:S(2)}) collective-permute-start(bf16[1664,256]{1,0:T(8,128)(2,1)S(1)} %bitcast.135), channel_id=1, source_target_pairs={{0,32},{32,0},{64,96},{96,64},{128,160},{160,128},{192,224},{224,1... | collective-permute-start | bytes 2555912 | tf_op jit(solution)/shard_map/ppermute | solution.py:78
  18.7 54.8 %collective-permute-start.7 = (bf16[256,1664]{1,0:T(8,128)(2,1)}, bf16[256,1664]{1,0:T(8,128)(2,1)}, u32[]{:S(2)}, u32[]{:S(2)}) collective-permute-start(bf16[256,1664]{1,0:T(8,128)(2,1)} %bitcast.22), channel_id=1, source_target_pairs={{0,32},{32,0},{64,96},{96,64},{128,160},{160,128},{192,224},{224,1... | collective-permute-start | bytes 2555912 | tf_op jit(solution)/shard_map/ppermute | solution.py:79
  23.1 46.0 %copy-start.6 = (bf16[1664,32]{0,1:T(8,128)(2,1)}, bf16[1664,32]{0,1:T(8,128)(2,1)S(1)}, u32[]{:S(2)}) copy-start(bf16[1664,32]{0,1:T(8,128)(2,1)S(1)} %get-tuple-element.25) | copy-start | bytes 319492
  23.1 46.0 %copy-start.8 = (bf16[1664,32]{0,1:T(8,128)(2,1)}, bf16[1664,32]{0,1:T(8,128)(2,1)S(1)}, u32[]{:S(2)}) copy-start(bf16[1664,32]{0,1:T(8,128)(2,1)S(1)} %get-tuple-element.27) | copy-start | bytes 319492
  28.5 13.4 %collective-permute-start = (bf16[64,1664]{1,0:T(8,128)(2,1)S(1)}, bf16[64,1664]{1,0:T(8,128)(2,1)S(1)}, u32[]{:S(2)}, u32[]{:S(2)}) collective-permute-start(bf16[64,1664]{1,0:T(8,128)(2,1)S(1)} %convolution_convert_fusion.3), channel_id=1, source_target_pairs={{0,64},{32,480},{64,128},{96,32},{128,192},{160,96},{192,256},{224... | collective-permute-start | bytes 638984 | tf_op jit(solution)/shard_map/ppermute | solution.py:96
  39.2 9.2 %collective-permute-start.1 = (bf16[64,1664]{1,0:T(8,128)(2,1)S(1)}, bf16[64,1664]{1,0:T(8,128)(2,1)S(1)}, u32[]{:S(2)}, u32[]{:S(2)}) collective-permute-start(bf16[64,1664]{1,0:T(8,128)(2,1)S(1)} %convolution_convert_fusion.3), channel_id=1, source_target_pairs={{0,448},{32,96},{64,0},{96,160},{128,64},{160,224},{192,128},{224,... | collective-permute-start | bytes 638984 | tf_op jit(solution)/shard_map/ppermute | solution.py:99
  41.3 27.9 %copy-start.11 = (bf16[1664,32]{0,1:T(8,128)(2,1)S(1)}, bf16[1664,32]{0,1:T(8,128)(2,1)}, u32[]{:S(2)}) copy-start(bf16[1664,32]{0,1:T(8,128)(2,1)} %get-tuple-element.26) | copy-start | bytes 319492
  42.0 8.5 %collective-permute-start.2 = (bf16[64,1664]{1,0:T(8,128)(2,1)S(1)}, bf16[64,1664]{1,0:T(8,128)(2,1)S(1)}, u32[]{:S(2)}, u32[]{:S(2)}) collective-permute-start(bf16[64,1664]{1,0:T(8,128)(2,1)S(1)} %collective-permute-done), channel_id=1, source_target_pairs={{0,64},{32,480},{64,128},{96,32},{128,192},{160,96},{192,256},{224... | collective-permute-start | bytes 638984 | tf_op jit(solution)/shard_map/ppermute | solution.py:96
  48.4 10.1 %collective-permute-start.3 = (bf16[64,1664]{1,0:T(8,128)(2,1)S(1)}, bf16[64,1664]{1,0:T(8,128)(2,1)S(1)}, u32[]{:S(2)}, u32[]{:S(2)}) collective-permute-start(bf16[64,1664]{1,0:T(8,128)(2,1)S(1)} %collective-permute-done.1), channel_id=1, source_target_pairs={{0,448},{32,96},{64,0},{96,160},{128,64},{160,224},{192,128},{224,... | collective-permute-start | bytes 638984 | tf_op jit(solution)/shard_map/ppermute | solution.py:99
  50.4 10.1 %collective-permute-start.4 = (bf16[64,1664]{1,0:T(8,128)(2,1)S(1)}, bf16[64,1664]{1,0:T(8,128)(2,1)S(1)}, u32[]{:S(2)}, u32[]{:S(2)}) collective-permute-start(bf16[64,1664]{1,0:T(8,128)(2,1)S(1)} %collective-permute-done.2), channel_id=1, source_target_pairs={{0,64},{32,480},{64,128},{96,32},{128,192},{160,96},{192,256},{224... | collective-permute-start | bytes 638984 | tf_op jit(solution)/shard_map/ppermute | solution.py:96
  58.5 9.2 %collective-permute-start.5 = (bf16[64,1664]{1,0:T(8,128)(2,1)S(1)}, bf16[64,1664]{1,0:T(8,128)(2,1)S(1)}, u32[]{:S(2)}, u32[]{:S(2)}) collective-permute-start(bf16[64,1664]{1,0:T(8,128)(2,1)S(1)} %collective-permute-done.3), channel_id=1, source_target_pairs={{0,448},{32,96},{64,0},{96,160},{128,64},{160,224},{192,128},{224,... | collective-permute-start | bytes 638984 | tf_op jit(solution)/shard_map/ppermute | solution.py:99
  60.5 8.6 %collective-permute-start.6 = (bf16[64,1664]{1,0:T(8,128)(2,1)S(1)}, bf16[64,1664]{1,0:T(8,128)(2,1)S(1)}, u32[]{:S(2)}, u32[]{:S(2)}) collective-permute-start(bf16[64,1664]{1,0:T(8,128)(2,1)S(1)} %collective-permute-done.4), channel_id=1, source_target_pairs={{0,64},{32,480},{64,128},{96,32},{128,192},{160,96},{192,256},{224... | collective-permute-start | bytes 638984 | tf_op jit(solution)/shard_map/ppermute | solution.py:96
  73.5 13.8 %copy-start.2 = (f32[256,256]{0,1:T(8,128)}, f32[256,256]{0,1:T(8,128)S(1)}, u32[]{:S(2)}) copy-start(f32[256,256]{0,1:T(8,128)S(1)} %get-tuple-element.37) | copy-start | bytes 786436
  75.2 12.6 %copy-start.4 = (f32[256,256]{0,1:T(8,128)}, f32[256,256]{0,1:T(8,128)S(1)}, u32[]{:S(2)}) copy-start(f32[256,256]{0,1:T(8,128)S(1)} %get-tuple-element.39) | copy-start | bytes 786436
  76.3 13.7 %collective-permute-start.9 = (bf16[256,128]{1,0:T(8,128)(2,1)S(1)}, bf16[256,128]{1,0:T(8,128)(2,1)S(1)}, u32[]{:S(2)}, u32[]{:S(2)}) collective-permute-start(bf16[256,128]{1,0:T(8,128)(2,1)S(1)} %convolution_convert_fusion.4), channel_id=1, source_target_pairs={{0,32},{32,0},{64,96},{96,64},{128,160},{160,128},{192,224},{224,1... | collective-permute-start | bytes 196616 | tf_op jit(solution)/shard_map/ppermute | solution.py:151
  87.8 1.8 %copy-start.7 = (bf16[1664,32]{0,1:T(8,128)(2,1)S(1)}, bf16[1664,32]{0,1:T(8,128)(2,1)}, u32[]{:S(2)}) copy-start(bf16[1664,32]{0,1:T(8,128)(2,1)} %copy-done.6) | copy-start | bytes 319492
  87.8 1.8 %copy-start.9 = (bf16[1664,32]{0,1:T(8,128)(2,1)S(1)}, bf16[1664,32]{0,1:T(8,128)(2,1)}, u32[]{:S(2)}) copy-start(bf16[1664,32]{0,1:T(8,128)(2,1)} %copy-done.8) | copy-start | bytes 319492
  90.3 5.4 %copy-start.5 = (f32[256,256]{0,1:T(8,128)S(1)}, f32[256,256]{0,1:T(8,128)}, u32[]{:S(2)}) copy-start(f32[256,256]{0,1:T(8,128)} %copy-done.4) | copy-start | bytes 786436
  91.3 30.7 %all-to-all-start.1 = ((bf16[8,32,1792]{2,1,0:T(8,128)(2,1)}), bf16[8,32,1792]{2,1,0:T(8,128)(2,1)}, u32[]{:S(2)}, u32[]{:S(2)}) async-start(bf16[8,32,1792]{2,1,0:T(8,128)(2,1)} %bitcast.134), calls=%async_computation.1 | async-start | bytes 1835008 | tf_op jit(solution)/shard_map/all_to_all | solution.py:159
  97.0 36.1 %collective-permute-start.10 = (bf16[1664,256]{1,0:T(8,128)(2,1)}, bf16[1664,256]{1,0:T(8,128)(2,1)}, u32[]{:S(2)}, u32[]{:S(2)}) collective-permute-start(bf16[1664,256]{1,0:T(8,128)(2,1)} %convolution_convert_fusion.1), channel_id=1, source_target_pairs={{0,32},{32,0},{64,96},{96,64},{128,160},{160,128},{192,224},{224,1... | collective-permute-start | bytes 2555912 | tf_op jit(solution)/shard_map/ppermute | solution.py:172
  100.3 30.3 %collective-permute-start.11 = (bf16[256,1664]{1,0:T(8,128)(2,1)}, bf16[256,1664]{1,0:T(8,128)(2,1)}, u32[]{:S(2)}, u32[]{:S(2)}) collective-permute-start(bf16[256,1664]{1,0:T(8,128)(2,1)} %convolution_convert_fusion), channel_id=1, source_target_pairs={{0,32},{32,0},{64,96},{96,64},{128,160},{160,128},{192,224},{224,1... | collective-permute-start | bytes 2555912 | tf_op jit(solution)/shard_map/ppermute | solution.py:173
  125.4 7.7 %copy-start.3 = (f32[256,256]{0,1:T(8,128)S(1)}, f32[256,256]{0,1:T(8,128)}, u32[]{:S(2)}) copy-start(f32[256,256]{0,1:T(8,128)} %copy-done.2) | copy-start | bytes 786436
  125.4 17.6 %all-to-all-start.2 = ((bf16[32,4,1664]{2,1,0:T(4,128)(2,1)}), bf16[32,4,1664]{2,1,0:T(4,128)(2,1)S(1)}, u32[]{:S(2)}, u32[]{:S(2)}) async-start(bf16[32,4,1664]{2,1,0:T(4,128)(2,1)} %reshape.230), calls=%async_computation.2 | async-start | bytes 851968 | tf_op jit(solution)/shard_map/all_to_all | solution.py:183
  144.0 15.2 %all-to-all-start.3 = ((bf16[16,2,1664]{2,1,0:T(2,128)(2,1)}), bf16[16,2,1664]{2,1,0:T(2,128)(2,1)S(1)}, u32[]{:S(2)}, u32[]{:S(2)}) async-start(bf16[16,2,1664]{2,1,0:T(2,128)(2,1)} %broadcast_in_dim.144), calls=%async_computation.3 | async-start | bytes 212992 | tf_op jit(solution)/shard_map/all_to_all | solution.py:194

commit v3 on v1

--- a/solution.py
+++ b/solution.py
@@ -45,6 +45,7 @@
     tok_count, width = tokens.shape
     plan = picks[0]
     cap = plan.shape[1]
+    hidden = w_in.shape[2]
     block_in = w_in[0]
     block_out = w_out[0]
 
@@ -74,6 +75,13 @@
     place_x = owner * (2 * SLOT) + rank
     pack = one_hot(jnp.concatenate([place_x, place_x + SLOT]), experts * 2 * SLOT)
     slab = dot_plain(pack, recv).astype(jnp.bfloat16)
+    swap = [(i, i ^ 1) for i in range(groups)]
+    partner_in = lax.ppermute(block_in, "dp", swap)
+    partner_out = lax.ppermute(block_out, "dp", swap)
+    both_in = jnp.concatenate([block_in, partner_in], axis=1)
+    both_out = jnp.concatenate([block_out, partner_out])
+    both_in, both_out = lax.optimization_barrier((both_in, both_out))
+
     chips = groups // 2
     here = lax.axis_index("dp") // 2
     shape = (chips, cap, width)
@@ -85,6 +93,8 @@
         if step == 0:
             arrived.append((slab, here))
         else:
+            if step == chips // 2:
+                early_x, early_dy = blocks_x, blocks_dy
             up = lax.ppermute(up, "dp", [(i, (i + 2) % groups) for i in range(groups)])
             arrived.append((up, (here - step) % chips))
             if step < chips // 2:
@@ -93,12 +103,6 @@
         for block, spot in arrived:
             blocks_x = lax.dynamic_update_slice(blocks_x, block[None, :cap], (spot, 0, 0))
             blocks_dy = lax.dynamic_update_slice(blocks_dy, block[None, cap:], (spot, 0, 0))
-    swap = [(i, i ^ 1) for i in range(groups)]
-    own_x = blocks_x.reshape(chips * cap, width)
-    own_dy = blocks_dy.reshape(chips * cap, width)
-    other_x = lax.ppermute(own_x, "dp", swap)
-    other_dy = lax.ppermute(own_dy, "dp", swap)
-
     router_parts = split_bf16(router, 3)
     router_wide = jnp.concatenate(router_parts, axis=1)
     router_back = jnp.concatenate([router_parts[0], router_parts[0], router_parts[1]], axis=1)
@@ -111,53 +115,52 @@
         ) + logit_parts[:, :experts]
         prob = jax.nn.softmax(logits, axis=-1)
         gate = jnp.sum(prob * mark, axis=-1, keepdims=True)
-        pre = dot_plain(rows_x, block_in)
+        pre = dot_plain(rows_x, both_in)
         cdf = 0.5 * (1.0 + lax.erf(pre * 0.7071067811865476))
         slope = cdf + pre * jnp.exp(-0.5 * pre * pre) * 0.3989422804014327
         act = (pre * cdf).astype(jnp.bfloat16)
-        dy_hidden = dot_cols(rows_dy, block_out)
+        dy_hidden = dot_cols(rows_dy, both_out)
         gate_part = jnp.sum(act.astype(jnp.float32) * dy_hidden, axis=-1, keepdims=True)
         pre_grad = (gate * dy_hidden * slope).astype(jnp.bfloat16)
         gated = (gate * act.astype(jnp.float32)).astype(jnp.bfloat16)
-        return pre_grad, gated, (gate_part * gate) * (mark - prob)
+
+        share_hi, share_lo = split_bf16((gate_part * gate) * (mark - prob), 2)
+        return pre_grad, gated, share_hi, share_lo
+
+    rows_x = blocks_x.reshape(chips * cap, width)
+    rows_dy = blocks_dy.reshape(chips * cap, width)
+    early = hidden_grads(early_x.reshape(chips * cap, width), early_dy.reshape(chips * cap, width))
+    late = hidden_grads(up[:cap], up[cap:])
+    hole = (here - chips // 2) % chips * cap
+    pre_grad, gated, share_hi, share_lo = (
+        lax.dynamic_update_slice(most, rest, (hole, 0)) for most, rest in zip(early, late)
+    )
 
     tiles = width // 128
     deal = experts * tiles // groups
-
-    def row_grads(pre_grad, share_hi, share_lo, extra):
-        left = jnp.concatenate([share_hi, share_lo, share_hi], axis=1)
-        rows = dot_cols(pre_grad, block_in) + dot_cols(left, router_back)
-        return jnp.concatenate([rows, extra], axis=1)
-
-    other_pre, other_gated, other_share = hidden_grads(other_x, other_dy)
-    own_pre, own_gated, own_share = hidden_grads(own_x, own_dy)
-    own_hi, own_lo = split_bf16(own_share, 2)
-    other_hi, other_lo = split_bf16(other_share, 2)
-    router_part = dot_rows(own_hi, own_x) + dot_rows(own_lo, own_x)
-    router_part += dot_rows(other_hi, other_x) + dot_rows(other_lo, other_x)
+    core = lax.axis_index("dp") % 2
+    row_id = jnp.arange(chips * cap, dtype=jnp.int32)
+    router_part = dot_rows(share_hi, rows_x) + dot_rows(share_lo, rows_x)
     router_part = router_part.astype(jnp.bfloat16)
     router_part = jnp.concatenate(
         [router_part[:, 128 * tile : 128 * (tile + 1)] for tile in range(tiles)]
     )
-    core = lax.axis_index("dp") % 2
-    row_id = jnp.arange(chips * cap, dtype=jnp.int32)
 
     def dealt(side):
         group, spot = 2 * (row_id // cap) + side, row_id % cap
         unit = spot % tiles * experts + SLOT * group + spot // tiles
-        pick = one_hot(jnp.where(row_id % cap < deal, unit, -1), experts * tiles)
+        pick = one_hot(jnp.where(spot < deal, unit, -1), experts * tiles)
         return dot_plain(pick, router_part)
 
-    own_extra, other_extra = dealt(core), dealt(1 - core)
-
-    other_rows = row_grads(other_pre, other_hi, other_lo, other_extra)
-    partner_rows = lax.ppermute(other_rows.astype(jnp.bfloat16), "dp", swap)
-    own_rows = row_grads(own_pre, own_hi, own_lo, own_extra)
-    own_rows = own_rows + partner_rows.astype(jnp.float32)
+    partner_extra = lax.ppermute(dealt(1 - core).astype(jnp.bfloat16), "dp", swap)
+    extra = (dealt(core) + partner_extra.astype(jnp.float32)).astype(jnp.bfloat16)
+
+    left = jnp.concatenate([share_hi, share_lo, share_hi], axis=1)
+    rows = (dot_cols(pre_grad, both_in) + dot_cols(left, router_back)).astype(jnp.bfloat16)
+    rows = jnp.concatenate([rows, extra], axis=1).reshape(chips, cap, width + 128)
     columns = [[i for i in range(groups) if i % 2 == side] for side in range(2)]
-    own_rows = own_rows.astype(jnp.bfloat16).reshape(chips, cap, width + 128)
     pieces = lax.all_to_all(
-        own_rows,
+        rows,
         "dp",
         split_axis=0,
         concat_axis=0,
@@ -167,8 +170,12 @@
     router_rows = jnp.sum(pieces[:, :deal, width:].astype(jnp.float32), axis=0)
     router_rows = router_rows.reshape(SLOT, width)
 
-    grad_in = dot_rows(own_x, own_pre) + dot_rows(other_x, other_pre)
-    grad_out = dot_rows(own_gated, own_dy) + dot_rows(other_gated, other_dy)
+    partner_in = dot_rows(rows_x, pre_grad[:, hidden:]).astype(jnp.bfloat16)
+    partner_out = dot_rows(gated[:, hidden:], rows_dy).astype(jnp.bfloat16)
+    partner_in = lax.ppermute(partner_in, "dp", swap)
+    partner_out = lax.ppermute(partner_out, "dp", swap)
+    grad_in = dot_rows(rows_x, pre_grad[:, :hidden]) + partner_in.astype(jnp.float32)
+    grad_out = dot_rows(gated[:, :hidden], rows_dy) + partner_out.astype(jnp.float32)
     grad_in, grad_out = grad_in.astype(jnp.bfloat16), grad_out.astype(jnp.bfloat16)
 
     slot = lax.broadcasted_iota(jnp.int32, (experts * 2 * SLOT, 1), 0) % (2 * SLOT)
@@ -185,9 +192,10 @@
     )
     router_rows = jnp.sum(ret[:, SLOT:].astype(jnp.float32), axis=0)
     grad_tokens = dot_rows(pick_x, ret.reshape(experts * 2 * SLOT, width)).astype(jnp.bfloat16)
+    router_rows = router_rows.astype(jnp.bfloat16)
     router_rows = jnp.broadcast_to(router_rows[None], (groups, SLOT, width))
     router_rows = lax.all_to_all(router_rows, "dp", split_axis=0, concat_axis=0, tiled=True)
-    grad_router = router_rows.reshape(experts, width).T
+    grad_router = router_rows.reshape(experts, width).astype(jnp.float32).T
     return grad_tokens, grad_in[None], grad_out[None], grad_router
 
 

time: 173 us -> 160 us (0.925)
  waiting for transfers between devices: 67.1 us -> 50.9 us
  starting transfers between devices: 69.6 us -> 72.9 us
  local copies, waits for them, and re-layouts: 9.02 us -> 6.33 us
  other arithmetic: 7.72 us -> 9.57 us
    all_to_all x1, waiting for transfers between devices: 26.3 us -> 19.2 us  [grads(): lax.all_to_all(rows, 'dp', split_axis=0, concat_axis=0, axis_index_groups...]
    all_to_all x1, waiting for transfers between devices: 9.84 us -> 4.42 us  [grads(): lax.all_to_all(send, 'expert', split_axis=0, concat_axis=0, tiled=True)]
    ppermute x3 -> x5, starting transfers between devices: 14.3 us -> 18.9 us  [the longest x1 9.76 us: grads(): lax.ppermute(dealt(1 - core).astype(jnp.bfloat16), 'dp', swap)]
    concatenate x1 -> x3, other arithmetic: 0.07 us -> 4.08 us  [the longest x1 1.54 us: grads(): both_out = jnp.concatenate([block_out, partner_out])]
    reshape x1 -> x0, local copies, waits for them, and re-layouts: 1.76 us -> none  [grads(): grad_router = router_rows.reshape(experts, width).T]
    dot_general x10 -> x8, matrix products: 9.02 us -> 9.74 us  [dot_rows(): lax.dot_general(left, right, (((0,), (0,)), ((), ())), preferred_element_...]
  transfers between devices with their start and end apart: 14 -> 16, of which waited for: 10 -> 8; matrix products, arithmetic and copies ran while one was open for 8% -> 11% of each run, Pallas kernels for 0% -> 0%
where the time goes in v3:
time: 160 us; the launch traced here: 159 us
  starting transfers between devices  72.9 us (46%)
  waiting for transfers between devices  50.9 us (32%)
  matrix products  17.6 us (11%)
  other arithmetic  9.57 us (6%)
  local copies, waits for them, and re-layouts  6.33 us (4%)
    ppermute x3, starting transfers between devices, grads(): lax.ppermute(down, 'dp', [(i, (i - 2) % groups) for i in range(groups)])  20.3 us
    all_to_all x1, waiting for transfers between devices, grads(): lax.all_to_all(rows, 'dp', split_axis=0, concat_axis=0, axis_index_groups...  19.2 us
    ppermute x4, waiting for transfers between devices, grads(): up = lax.ppermute(up, 'dp', [(i, (i + 2) % groups) for i in range(groups)])  11.6 us
    all_to_all x1, starting transfers between devices, grads(): lax.all_to_all(send, 'expert', split_axis=0, concat_axis=0, tiled=True)  10.5 us
    ppermute x1, starting transfers between devices, grads(): lax.ppermute(dealt(1 - core).astype(jnp.bfloat16), 'dp', swap)  9.76 us
    dot_general x8, matrix products, dot_rows(): lax.dot_general(left, right, (((0,), (0,)), ((), ())), preferred_element_...  9.74 us
    ppermute x4, starting transfers between devices, grads(): up = lax.ppermute(up, 'dp', [(i, (i + 2) % groups) for i in range(groups)])  7.67 us
    all_to_all x1, waiting for transfers between devices, grads(): lax.all_to_all(router_rows, 'dp', split_axis=0, concat_axis=0, tiled=True)  7.41 us
  transfers between devices with their start and end apart: 16, of which 8 were waited for; matrix products, arithmetic and copies ran while one was open for 11% of the time, Pallas kernels for 0%

profile of v3, /device:TPU:1, one launch (start us, length us, event | category | flops | bytes accessed | tf_op | source)
XLA Modules:
  0.0 158.8 jit_solution(13030336864049996502)
XLA Ops:
  0.7 0.7 maximum_convert_fusion
  1.4 0.9 fusion.81
  3.5 1.4 fusion.6
  5.0 0.9 reshape.235
  5.8 10.5 %all-to-all-start = ((bf16[32,4,1664]{2,1,0:T(4,128)(2,1)}), bf16[32,4,1664]{2,1,0:T(4,128)(2,1)S(1)}, u32[]{:S(2)}, u32[]{:S(2)}) async-start(bf16[32,4,1664]{2,1,0:T(4,128)(2,1)} %reshape.235), calls=%async_computation | async-start | bytes 851968 | tf_op jit(solution)/shard_map/all_to_all | solution.py:67
  16.3 2.9 %collective-permute-start.6 = (bf16[1664,256]{1,0:T(8,128)(2,1)S(1)}, bf16[1664,256]{1,0:T(8,128)(2,1)}, u32[]{:S(2)}, u32[]{:S(2)}) collective-permute-start(bf16[1664,256]{1,0:T(8,128)(2,1)S(1)} %bitcast.125), channel_id=1, source_target_pairs={{0,32},{32,0},{64,96},{96,64},{128,160},{160,128},{192,224},{224,1... | collective-permute-start | bytes 2555912 | tf_op jit(solution)/shard_map/ppermute | solution.py:79
  19.2 1.9 %collective-permute-start.7 = (bf16[256,1664]{1,0:T(8,128)(2,1)}, bf16[256,1664]{1,0:T(8,128)(2,1)}, u32[]{:S(2)}, u32[]{:S(2)}) collective-permute-start(bf16[256,1664]{1,0:T(8,128)(2,1)} %bitcast.21), channel_id=1, source_target_pairs={{0,32},{32,0},{64,96},{96,64},{128,160},{160,128},{192,224},{224,1... | collective-permute-start | bytes 2555912 | tf_op jit(solution)/shard_map/ppermute | solution.py:80
  21.2 0.7 and_select_fusion.7
  21.9 0.8 broadcast_add_fusion
  23.0 0.6 add_select_fusion.1
  23.5 0.6 add_select_fusion
  24.2 4.4 %all-to-all-done = bf16[32,4,1664]{2,1,0:T(4,128)(2,1)S(1)} async-done(((bf16[32,4,1664]{2,1,0:T(4,128)(2,1)}), bf16[32,4,1664]{2,1,0:T(4,128)(2,1)S(1)}, u32[]{:S(2)}, u32[]{:S(2)}) %all-to-all-start) | async-done | bytes 426016 | tf_op jit(solution)/shard_map/all_to_all | solution.py:67
  29.0 10.7 %collective-permute-start.1 = (bf16[64,1664]{1,0:T(8,128)(2,1)S(1)}, bf16[64,1664]{1,0:T(8,128)(2,1)S(1)}, u32[]{:S(2)}, u32[]{:S(2)}) collective-permute-start(bf16[64,1664]{1,0:T(8,128)(2,1)S(1)} %convolution_convert_fusion.3), channel_id=1, source_target_pairs={{0,448},{32,480},{64,0},{96,32},{128,64},{160,96},{192,128},{224,1... | collective-permute-start | bytes 638984 | tf_op jit(solution)/shard_map/ppermute | solution.py:101
  39.7 1.9 %collective-permute-start = (bf16[64,1664]{1,0:T(8,128)(2,1)S(1)}, bf16[64,1664]{1,0:T(8,128)(2,1)S(1)}, u32[]{:S(2)}, u32[]{:S(2)}) collective-permute-start(bf16[64,1664]{1,0:T(8,128)(2,1)S(1)} %convolution_convert_fusion.3), channel_id=1, source_target_pairs={{0,64},{32,96},{64,128},{96,160},{128,192},{160,224},{192,256},{22... | collective-permute-start | bytes 638984 | tf_op jit(solution)/shard_map/ppermute | solution.py:98
  41.8 1.5 pad_maximum_fusion
  43.4 1.5 pad_maximum_fusion.1
  44.9 4.6 %collective-permute-start.3 = (bf16[64,1664]{1,0:T(8,128)(2,1)S(1)}, bf16[64,1664]{1,0:T(8,128)(2,1)S(1)}, u32[]{:S(2)}, u32[]{:S(2)}) collective-permute-start(bf16[64,1664]{1,0:T(8,128)(2,1)S(1)} %collective-permute-done.1), channel_id=1, source_target_pairs={{0,448},{32,480},{64,0},{96,32},{128,64},{160,96},{192,128},{224,1... | collective-permute-start | bytes 638984 | tf_op jit(solution)/shard_map/ppermute | solution.py:101
  49.5 1.9 %collective-permute-start.2 = (bf16[64,1664]{1,0:T(8,128)(2,1)S(1)}, bf16[64,1664]{1,0:T(8,128)(2,1)S(1)}, u32[]{:S(2)}, u32[]{:S(2)}) collective-permute-start(bf16[64,1664]{1,0:T(8,128)(2,1)S(1)} %collective-permute-done), channel_id=1, source_target_pairs={{0,64},{32,96},{64,128},{96,160},{128,192},{160,224},{192,256},{22... | collective-permute-start | bytes 638984 | tf_op jit(solution)/shard_map/ppermute | solution.py:98
  51.5 0.8 collective-permute-done.3
  52.3 5.0 %collective-permute-start.5 = (bf16[64,1664]{1,0:T(8,128)(2,1)S(1)}, bf16[64,1664]{1,0:T(8,128)(2,1)S(1)}, u32[]{:S(2)}, u32[]{:S(2)}) collective-permute-start(bf16[64,1664]{1,0:T(8,128)(2,1)S(1)} %collective-permute-done.3), channel_id=1, source_target_pairs={{0,448},{32,480},{64,0},{96,32},{128,64},{160,96},{192,128},{224,1... | collective-permute-start | bytes 638984 | tf_op jit(solution)/shard_map/ppermute | solution.py:101
  57.3 1.9 %collective-permute-start.4 = (bf16[64,1664]{1,0:T(8,128)(2,1)S(1)}, bf16[64,1664]{1,0:T(8,128)(2,1)S(1)}, u32[]{:S(2)}, u32[]{:S(2)}) collective-permute-start(bf16[64,1664]{1,0:T(8,128)(2,1)S(1)} %collective-permute-done.2), channel_id=1, source_target_pairs={{0,64},{32,96},{64,128},{96,160},{128,192},{160,224},{192,256},{22... | collective-permute-start | bytes 638984 | tf_op jit(solution)/shard_map/ppermute | solution.py:98
  59.3 5.8 %collective-permute-done.4 = bf16[64,1664]{1,0:T(8,128)(2,1)S(1)} collective-permute-done((bf16[64,1664]{1,0:T(8,128)(2,1)S(1)}, bf16[64,1664]{1,0:T(8,128)(2,1)S(1)}, u32[]{:S(2)}, u32[]{:S(2)}) %collective-permute-start.4) | collective-permute-done | bytes 213024 | tf_op jit(solution)/shard_map/ppermute | solution.py:98
  65.8 0.7 fusion.101
  66.5 0.9 fusion.10
  67.5 1.9 %collective-permute-start.8 = (bf16[64,1664]{1,0:T(8,128)(2,1)S(1)}, bf16[64,1664]{1,0:T(8,128)(2,1)S(1)}, u32[]{:S(2)}, u32[]{:S(2)}) collective-permute-start(bf16[64,1664]{1,0:T(8,128)(2,1)S(1)} %collective-permute-done.4), channel_id=1, source_target_pairs={{0,64},{32,96},{64,128},{96,160},{128,192},{160,224},{192,256},{22... | collective-permute-start | bytes 638984 | tf_op jit(solution)/shard_map/ppermute | solution.py:98
  69.5 5.8 %collective-permute-done.8 = bf16[64,1664]{1,0:T(8,128)(2,1)S(1)} collective-permute-done((bf16[64,1664]{1,0:T(8,128)(2,1)S(1)}, bf16[64,1664]{1,0:T(8,128)(2,1)S(1)}, u32[]{:S(2)}, u32[]{:S(2)}) %collective-permute-start.8) | collective-permute-done | bytes 213024 | tf_op jit(solution)/shard_map/ppermute | solution.py:98
  75.7 0.6 fusion.51
  77.7 0.7 bitcast_dynamic-update-slice_fusion
  78.7 1.4 fusion.21
  80.8 9.8 %collective-permute-start.9 = (bf16[256,128]{1,0:T(8,128)(2,1)S(1)}, bf16[256,128]{1,0:T(8,128)(2,1)S(1)}, u32[]{:S(2)}, u32[]{:S(2)}) collective-permute-start(bf16[256,128]{1,0:T(8,128)(2,1)S(1)} %convolution_convert_fusion.4), channel_id=1, source_target_pairs={{0,32},{32,0},{64,96},{96,64},{128,160},{160,128},{192,224},{224,1... | collective-permute-start | bytes 196616 | tf_op jit(solution)/shard_map/ppermute | solution.py:155
  90.6 0.7 fusion.2
  91.7 1.0 pad_maximum_fusion.2
  92.7 3.7 %all-to-all-start.1 = ((bf16[8,32,1792]{2,1,0:T(8,128)(2,1)}), bf16[8,32,1792]{2,1,0:T(8,128)(2,1)S(1)}, u32[]{:S(2)}, u32[]{:S(2)}) async-start(bf16[8,32,1792]{2,1,0:T(8,128)(2,1)} %bitcast.24), calls=%async_computation.1 | async-start | bytes 1835008 | tf_op jit(solution)/shard_map/all_to_all | solution.py:162
  96.5 1.3 convolution_convert_fusion.1
  97.9 2.3 %collective-permute-start.10 = (bf16[1664,256]{1,0:T(8,128)(2,1)}, bf16[1664,256]{1,0:T(8,128)(2,1)}, u32[]{:S(2)}, u32[]{:S(2)}) collective-permute-start(bf16[1664,256]{1,0:T(8,128)(2,1)} %convolution_convert_fusion.1), channel_id=1, source_target_pairs={{0,32},{32,0},{64,96},{96,64},{128,160},{160,128},{192,224},{224,1... | collective-permute-start | bytes 2555912 | tf_op jit(solution)/shard_map/ppermute | solution.py:175
  100.2 1.3 convolution_convert_fusion
  101.5 2.1 %collective-permute-start.11 = (bf16[256,1664]{1,0:T(8,128)(2,1)}, bf16[256,1664]{1,0:T(8,128)(2,1)}, u32[]{:S(2)}, u32[]{:S(2)}) collective-permute-start(bf16[256,1664]{1,0:T(8,128)(2,1)} %convolution_convert_fusion), channel_id=1, source_target_pairs={{0,32},{32,0},{64,96},{96,64},{128,160},{160,128},{192,224},{224,1... | collective-permute-start | bytes 2555912 | tf_op jit(solution)/shard_map/ppermute | solution.py:176
  103.6 19.2 %all-to-all-done.1 = bf16[8,32,1792]{2,1,0:T(8,128)(2,1)S(1)} async-done(((bf16[8,32,1792]{2,1,0:T(8,128)(2,1)}), bf16[8,32,1792]{2,1,0:T(8,128)(2,1)S(1)}, u32[]{:S(2)}, u32[]{:S(2)}) %all-to-all-start.1) | async-done | bytes 917536 | tf_op jit(solution)/shard_map/all_to_all | solution.py:162
  123.3 0.9 reshape.242
  124.1 5.4 %all-to-all-start.2 = ((bf16[32,4,1664]{2,1,0:T(4,128)(2,1)}), bf16[32,4,1664]{2,1,0:T(4,128)(2,1)S(1)}, u32[]{:S(2)}, u32[]{:S(2)}) async-start(bf16[32,4,1664]{2,1,0:T(4,128)(2,1)} %reshape.242), calls=%async_computation.2 | async-start | bytes 851968 | tf_op jit(solution)/shard_map/all_to_all | solution.py:186
  129.6 2.5 %fusion.4 = bf16[1,256,1664]{2,1,0:T(8,128)(2,1)} fusion(bf16[256,1664]{1,0:T(8,128)(2,1)S(1)} %bitcast.122, bf16[256,1664]{1,0:T(8,128)(2,1)} %collective-permute-done.11, bf16[256,512]{1,0:T(8,128)(2,1)S(1)} %copy-done.10), kind=kOutput, calls=%fused_computation.11 | convolution fusion | flops 219381760 | bytes 2686976 | tf_op jit(solution)/shard_map/dot_general | solution.py:11
  132.1 2.5 %fusion.5 = bf16[1,1664,256]{2,1,0:T(8,128)(2,1)} fusion(bf16[256,1664]{1,0:T(8,128)(2,1)S(1)} %bitcast.119, bf16[1664,256]{1,0:T(8,128)(2,1)} %collective-permute-done.10, bf16[256,512]{1,0:T(8,128)(2,1)S(1)} %get-tuple-element.39), kind=kOutput, calls=%fused_computation.12 | convolution fusion | flops 219381760 | bytes 2686976 | tf_op jit(solution)/shard_map/dot_general | solution.py:11
  134.6 7.3 %all-to-all-done.2 = bf16[32,4,1664]{2,1,0:T(4,128)(2,1)S(1)} async-done(((bf16[32,4,1664]{2,1,0:T(4,128)(2,1)}), bf16[32,4,1664]{2,1,0:T(4,128)(2,1)S(1)}, u32[]{:S(2)}, u32[]{:S(2)}) %all-to-all-start.2) | async-done | bytes 426016 | tf_op jit(solution)/shard_map/all_to_all | solution.py:186
  142.2 0.7 broadcast_in_dim.147
  142.9 6.5 %all-to-all-start.3 = ((bf16[16,2,1664]{2,1,0:T(2,128)(2,1)}), bf16[16,2,1664]{2,1,0:T(2,128)(2,1)S(1)}, u32[]{:S(2)}, u32[]{:S(2)}) async-start(bf16[16,2,1664]{2,1,0:T(2,128)(2,1)} %broadcast_in_dim.147), calls=%async_computation.3 | async-start | bytes 212992 | tf_op jit(solution)/shard_map/all_to_all | solution.py:197
  149.6 1.1 convolution_convert_fusion.2
  150.7 7.4 %all-to-all-done.3 = bf16[16,2,1664]{2,1,0:T(2,128)(2,1)S(1)} async-done(((bf16[16,2,1664]{2,1,0:T(2,128)(2,1)}), bf16[16,2,1664]{2,1,0:T(2,128)(2,1)S(1)}, u32[]{:S(2)}, u32[]{:S(2)}) %all-to-all-start.3) | async-done | bytes 106528 | tf_op jit(solution)/shard_map/all_to_all | solution.py:197
  158.1 0.7 reshape.245
  (120 shorter events, 7.1 us)
Async XLA Ops:
  0.6 2.6 %copy-start = (bf16[128,1664]{1,0:T(8,128)(2,1)S(1)}, bf16[128,1664]{1,0:T(8,128)(2,1)}, u32[]{:S(2)}) copy-start(bf16[128,1664]{1,0:T(8,128)(2,1)} %param.7) | copy-start | bytes 1277956
  2.7 0.5 copy-start.16
  3.5 12.8 %copy-start.3 = (bf16[1,1664,256]{2,1,0:T(8,128)(2,1)S(1)}, bf16[1,1664,256]{2,1,0:T(8,128)(2,1)}, u32[]{:S(2)}) copy-start(bf16[1,1664,256]{2,1,0:T(8,128)(2,1)} %param.12) | copy-start | bytes 2555908
  5.0 19.2 %copy-start.11 = (f32[1664,32]{0,1:T(8,128)S(1)}, f32[1664,32]{0,1:T(8,128)}, u32[]{:S(2)}) copy-start(f32[1664,32]{0,1:T(8,128)} %param.11) | copy-start | bytes 638980
  5.8 22.8 %all-to-all-start = ((bf16[32,4,1664]{2,1,0:T(4,128)(2,1)}), bf16[32,4,1664]{2,1,0:T(4,128)(2,1)S(1)}, u32[]{:S(2)}, u32[]{:S(2)}) async-start(bf16[32,4,1664]{2,1,0:T(4,128)(2,1)} %reshape.235), calls=%async_computation | async-start | bytes 851968 | tf_op jit(solution)/shard_map/all_to_all | solution.py:67
  16.3 25.5 %collective-permute-start.6 = (bf16[1664,256]{1,0:T(8,128)(2,1)S(1)}, bf16[1664,256]{1,0:T(8,128)(2,1)}, u32[]{:S(2)}, u32[]{:S(2)}) collective-permute-start(bf16[1664,256]{1,0:T(8,128)(2,1)S(1)} %bitcast.125), channel_id=1, source_target_pairs={{0,32},{32,0},{64,96},{96,64},{128,160},{160,128},{192,224},{224,1... | collective-permute-start | bytes 2555912 | tf_op jit(solution)/shard_map/ppermute | solution.py:79
  19.2 24.2 %collective-permute-start.7 = (bf16[256,1664]{1,0:T(8,128)(2,1)}, bf16[256,1664]{1,0:T(8,128)(2,1)}, u32[]{:S(2)}, u32[]{:S(2)}) collective-permute-start(bf16[256,1664]{1,0:T(8,128)(2,1)} %bitcast.21), channel_id=1, source_target_pairs={{0,32},{32,0},{64,96},{96,64},{128,160},{160,128},{192,224},{224,1... | collective-permute-start | bytes 2555912 | tf_op jit(solution)/shard_map/ppermute | solution.py:80
  22.7 1.5 copy-start.18
  22.7 43.0 %copy-start.14 = (f32[32]{0:T(128)}, f32[32]{0:T(128)S(1)}, u32[]{:S(2)}) copy-start(f32[32]{0:T(128)S(1)} %compare_convert_fusion) | copy-start | bytes 388
  24.2 41.0 %copy-start.4 = (bf16[1664,32]{0,1:T(8,128)(2,1)}, bf16[1664,32]{0,1:T(8,128)(2,1)S(1)}, u32[]{:S(2)}) copy-start(bf16[1664,32]{0,1:T(8,128)(2,1)S(1)} %get-tuple-element.24) | copy-start | bytes 319492
  24.2 41.0 %copy-start.6 = (bf16[1664,32]{0,1:T(8,128)(2,1)}, bf16[1664,32]{0,1:T(8,128)(2,1)S(1)}, u32[]{:S(2)}) copy-start(bf16[1664,32]{0,1:T(8,128)(2,1)S(1)} %get-tuple-element.26) | copy-start | bytes 319492
  24.2 41.0 %copy-start.12 = (bf16[1664,32]{0,1:T(8,128)(2,1)}, bf16[1664,32]{0,1:T(8,128)(2,1)S(1)}, u32[]{:S(2)}) copy-start(bf16[1664,32]{0,1:T(8,128)(2,1)S(1)} %get-tuple-element.25) | copy-start | bytes 319492
  29.0 15.9 %collective-permute-start.1 = (bf16[64,1664]{1,0:T(8,128)(2,1)S(1)}, bf16[64,1664]{1,0:T(8,128)(2,1)S(1)}, u32[]{:S(2)}, u32[]{:S(2)}) collective-permute-start(bf16[64,1664]{1,0:T(8,128)(2,1)S(1)} %convolution_convert_fusion.3), channel_id=1, source_target_pairs={{0,448},{32,480},{64,0},{96,32},{128,64},{160,96},{192,128},{224,1... | collective-permute-start | bytes 638984 | tf_op jit(solution)/shard_map/ppermute | solution.py:101
  39.7 9.8 %collective-permute-start = (bf16[64,1664]{1,0:T(8,128)(2,1)S(1)}, bf16[64,1664]{1,0:T(8,128)(2,1)S(1)}, u32[]{:S(2)}, u32[]{:S(2)}) collective-permute-start(bf16[64,1664]{1,0:T(8,128)(2,1)S(1)} %convolution_convert_fusion.3), channel_id=1, source_target_pairs={{0,64},{32,96},{64,128},{96,160},{128,192},{160,224},{192,256},{22... | collective-permute-start | bytes 638984 | tf_op jit(solution)/shard_map/ppermute | solution.py:98
  44.9 7.3 %collective-permute-start.3 = (bf16[64,1664]{1,0:T(8,128)(2,1)S(1)}, bf16[64,1664]{1,0:T(8,128)(2,1)S(1)}, u32[]{:S(2)}, u32[]{:S(2)}) collective-permute-start(bf16[64,1664]{1,0:T(8,128)(2,1)S(1)} %collective-permute-done.1), channel_id=1, source_target_pairs={{0,448},{32,480},{64,0},{96,32},{128,64},{160,96},{192,128},{224,1... | collective-permute-start | bytes 638984 | tf_op jit(solution)/shard_map/ppermute | solution.py:101
  49.5 7.8 %collective-permute-start.2 = (bf16[64,1664]{1,0:T(8,128)(2,1)S(1)}, bf16[64,1664]{1,0:T(8,128)(2,1)S(1)}, u32[]{:S(2)}, u32[]{:S(2)}) collective-permute-start(bf16[64,1664]{1,0:T(8,128)(2,1)S(1)} %collective-permute-done), channel_id=1, source_target_pairs={{0,64},{32,96},{64,128},{96,160},{128,192},{160,224},{192,256},{22... | collective-permute-start | bytes 638984 | tf_op jit(solution)/shard_map/ppermute | solution.py:98
  52.3 12.9 %collective-permute-start.5 = (bf16[64,1664]{1,0:T(8,128)(2,1)S(1)}, bf16[64,1664]{1,0:T(8,128)(2,1)S(1)}, u32[]{:S(2)}, u32[]{:S(2)}) collective-permute-start(bf16[64,1664]{1,0:T(8,128)(2,1)S(1)} %collective-permute-done.3), channel_id=1, source_target_pairs={{0,448},{32,480},{64,0},{96,32},{128,64},{160,96},{192,128},{224,1... | collective-permute-start | bytes 638984 | tf_op jit(solution)/shard_map/ppermute | solution.py:101
  57.3 7.8 %collective-permute-start.4 = (bf16[64,1664]{1,0:T(8,128)(2,1)S(1)}, bf16[64,1664]{1,0:T(8,128)(2,1)S(1)}, u32[]{:S(2)}, u32[]{:S(2)}) collective-permute-start(bf16[64,1664]{1,0:T(8,128)(2,1)S(1)} %collective-permute-done.2), channel_id=1, source_target_pairs={{0,64},{32,96},{64,128},{96,160},{128,192},{160,224},{192,256},{22... | collective-permute-start | bytes 638984 | tf_op jit(solution)/shard_map/ppermute | solution.py:98
  65.2 1.3 copy-start.1
  66.5 3.0 %copy-start.15 = (f32[32]{0:T(128)S(1)}, f32[32]{0:T(128)}, u32[]{:S(2)}) copy-start(f32[32]{0:T(128)} %copy-done.14) | copy-start | bytes 388
  66.5 8.8 %copy-start.5 = (bf16[1664,32]{0,1:T(8,128)(2,1)S(1)}, bf16[1664,32]{0,1:T(8,128)(2,1)}, u32[]{:S(2)}) copy-start(bf16[1664,32]{0,1:T(8,128)(2,1)} %copy-done.4) | copy-start | bytes 319492
  66.5 8.8 %copy-start.7 = (bf16[1664,32]{0,1:T(8,128)(2,1)S(1)}, bf16[1664,32]{0,1:T(8,128)(2,1)}, u32[]{:S(2)}) copy-start(bf16[1664,32]{0,1:T(8,128)(2,1)} %copy-done.6) | copy-start | bytes 319492
  66.5 8.8 %copy-start.13 = (bf16[1664,32]{0,1:T(8,128)(2,1)S(1)}, bf16[1664,32]{0,1:T(8,128)(2,1)}, u32[]{:S(2)}) copy-start(bf16[1664,32]{0,1:T(8,128)(2,1)} %copy-done.12) | copy-start | bytes 319492
  67.5 7.8 %collective-permute-start.8 = (bf16[64,1664]{1,0:T(8,128)(2,1)S(1)}, bf16[64,1664]{1,0:T(8,128)(2,1)S(1)}, u32[]{:S(2)}, u32[]{:S(2)}) collective-permute-start(bf16[64,1664]{1,0:T(8,128)(2,1)S(1)} %collective-permute-done.4), channel_id=1, source_target_pairs={{0,64},{32,96},{64,128},{96,160},{128,192},{160,224},{192,256},{22... | collective-permute-start | bytes 638984 | tf_op jit(solution)/shard_map/ppermute | solution.py:98
  76.8 0.7 copy-start.8
  78.7 1.9 %copy-start.21 = (s32[256]{0:T(256)S(1)}, s32[256]{0:T(256)}, u32[]{:S(2)}) copy-start(s32[256]{0:T(256)} %add_select_fusion) | copy-start | bytes 3076
  80.8 10.6 %collective-permute-start.9 = (bf16[256,128]{1,0:T(8,128)(2,1)S(1)}, bf16[256,128]{1,0:T(8,128)(2,1)S(1)}, u32[]{:S(2)}, u32[]{:S(2)}) collective-permute-start(bf16[256,128]{1,0:T(8,128)(2,1)S(1)} %convolution_convert_fusion.4), channel_id=1, source_target_pairs={{0,32},{32,0},{64,96},{96,64},{128,160},{160,128},{192,224},{224,1... | collective-permute-start | bytes 196616 | tf_op jit(solution)/shard_map/ppermute | solution.py:155
  90.6 0.9 copy-start.20
  91.7 4.7 %copy-start.19 = (s32[32]{0:T(128)S(1)}, s32[32]{0:T(128)}, u32[]{:S(2)}) copy-start(s32[32]{0:T(128)} %copy-done.18) | copy-start | bytes 388
  92.7 7.4 %copy-start.2 = (bf16[8,32,1664]{2,1,0:T(8,128)(2,1)S(1)}, bf16[8,32,1664]{2,1,0:T(8,128)(2,1)}, u32[]{:S(2)}) copy-start(bf16[8,32,1664]{2,1,0:T(8,128)(2,1)} %get-tuple-element.22) | copy-start | bytes 2555908
  92.7 30.0 %all-to-all-start.1 = ((bf16[8,32,1792]{2,1,0:T(8,128)(2,1)}), bf16[8,32,1792]{2,1,0:T(8,128)(2,1)S(1)}, u32[]{:S(2)}, u32[]{:S(2)}) async-start(bf16[8,32,1792]{2,1,0:T(8,128)(2,1)} %bitcast.24), calls=%async_computation.1 | async-start | bytes 1835008 | tf_op jit(solution)/shard_map/all_to_all | solution.py:162
  96.5 3.6 %copy-start.9 = (bf16[256,512]{1,0:T(8,128)(2,1)S(1)}, bf16[256,512]{1,0:T(8,128)(2,1)}, u32[]{:S(2)}) copy-start(bf16[256,512]{1,0:T(8,128)(2,1)} %copy-done.8) | copy-start | bytes 786436
  97.9 34.2 %collective-permute-start.10 = (bf16[1664,256]{1,0:T(8,128)(2,1)}, bf16[1664,256]{1,0:T(8,128)(2,1)}, u32[]{:S(2)}, u32[]{:S(2)}) collective-permute-start(bf16[1664,256]{1,0:T(8,128)(2,1)} %convolution_convert_fusion.1), channel_id=1, source_target_pairs={{0,32},{32,0},{64,96},{96,64},{128,160},{160,128},{192,224},{224,1... | collective-permute-start | bytes 2555912 | tf_op jit(solution)/shard_map/ppermute | solution.py:175
  101.5 28.1 %collective-permute-start.11 = (bf16[256,1664]{1,0:T(8,128)(2,1)}, bf16[256,1664]{1,0:T(8,128)(2,1)}, u32[]{:S(2)}, u32[]{:S(2)}) collective-permute-start(bf16[256,1664]{1,0:T(8,128)(2,1)} %convolution_convert_fusion), channel_id=1, source_target_pairs={{0,32},{32,0},{64,96},{96,64},{128,160},{160,128},{192,224},{224,1... | collective-permute-start | bytes 2555912 | tf_op jit(solution)/shard_map/ppermute | solution.py:176
  122.8 6.7 %copy-start.10 = (bf16[256,512]{1,0:T(8,128)(2,1)S(1)}, bf16[256,512]{1,0:T(8,128)(2,1)}, u32[]{:S(2)}) copy-start(bf16[256,512]{1,0:T(8,128)(2,1)} %copy-done.8) | copy-start | bytes 786436
  124.1 17.8 %all-to-all-start.2 = ((bf16[32,4,1664]{2,1,0:T(4,128)(2,1)}), bf16[32,4,1664]{2,1,0:T(4,128)(2,1)S(1)}, u32[]{:S(2)}, u32[]{:S(2)}) async-start(bf16[32,4,1664]{2,1,0:T(4,128)(2,1)} %reshape.242), calls=%async_computation.2 | async-start | bytes 851968 | tf_op jit(solution)/shard_map/all_to_all | solution.py:186
  132.1 17.5 %copy-start.17 = (s32[128]{0:T(128)S(1)}, s32[128]{0:T(128)}, u32[]{:S(2)}) copy-start(s32[128]{0:T(128)} %copy-done.16) | copy-start | bytes 1540
  142.9 15.2 %all-to-all-start.3 = ((bf16[16,2,1664]{2,1,0:T(2,128)(2,1)}), bf16[16,2,1664]{2,1,0:T(2,128)(2,1)S(1)}, u32[]{:S(2)}, u32[]{:S(2)}) async-start(bf16[16,2,1664]{2,1,0:T(2,128)(2,1)} %broadcast_in_dim.147), calls=%async_computation.3 | async-start | bytes 212992 | tf_op jit(solution)/shard_map/all_to_all | solution.py:197

commit v4 on v3

--- a/solution.py
+++ b/solution.py
@@ -93,8 +93,6 @@
         if step == 0:
             arrived.append((slab, here))
         else:
-            if step == chips // 2:
-                early_x, early_dy = blocks_x, blocks_dy
             up = lax.ppermute(up, "dp", [(i, (i + 2) % groups) for i in range(groups)])
             arrived.append((up, (here - step) % chips))
             if step < chips // 2:
@@ -103,38 +101,30 @@
         for block, spot in arrived:
             blocks_x = lax.dynamic_update_slice(blocks_x, block[None, :cap], (spot, 0, 0))
             blocks_dy = lax.dynamic_update_slice(blocks_dy, block[None, cap:], (spot, 0, 0))
+    rows_x = blocks_x.reshape(chips * cap, width)
+    rows_dy = blocks_dy.reshape(chips * cap, width)
+
     router_parts = split_bf16(router, 3)
     router_wide = jnp.concatenate(router_parts, axis=1)
     router_back = jnp.concatenate([router_parts[0], router_parts[0], router_parts[1]], axis=1)
     mark = (lax.broadcasted_iota(jnp.int32, (1, experts), 1) == me).astype(jnp.float32)
 
-    def hidden_grads(rows_x, rows_dy):
-        logit_parts = dot_plain(rows_x, router_wide)
-        logits = (
-            logit_parts[:, 2 * experts :] + logit_parts[:, experts : 2 * experts]
-        ) + logit_parts[:, :experts]
-        prob = jax.nn.softmax(logits, axis=-1)
-        gate = jnp.sum(prob * mark, axis=-1, keepdims=True)
-        pre = dot_plain(rows_x, both_in)
-        cdf = 0.5 * (1.0 + lax.erf(pre * 0.7071067811865476))
-        slope = cdf + pre * jnp.exp(-0.5 * pre * pre) * 0.3989422804014327
-        act = (pre * cdf).astype(jnp.bfloat16)
-        dy_hidden = dot_cols(rows_dy, both_out)
-        gate_part = jnp.sum(act.astype(jnp.float32) * dy_hidden, axis=-1, keepdims=True)
-        pre_grad = (gate * dy_hidden * slope).astype(jnp.bfloat16)
-        gated = (gate * act.astype(jnp.float32)).astype(jnp.bfloat16)
-
-        share_hi, share_lo = split_bf16((gate_part * gate) * (mark - prob), 2)
-        return pre_grad, gated, share_hi, share_lo
-
-    rows_x = blocks_x.reshape(chips * cap, width)
-    rows_dy = blocks_dy.reshape(chips * cap, width)
-    early = hidden_grads(early_x.reshape(chips * cap, width), early_dy.reshape(chips * cap, width))
-    late = hidden_grads(up[:cap], up[cap:])
-    hole = (here - chips // 2) % chips * cap
-    pre_grad, gated, share_hi, share_lo = (
-        lax.dynamic_update_slice(most, rest, (hole, 0)) for most, rest in zip(early, late)
-    )
+    logit_parts = dot_plain(rows_x, router_wide)
+    logits = (
+        logit_parts[:, 2 * experts :] + logit_parts[:, experts : 2 * experts]
+    ) + logit_parts[:, :experts]
+    prob = jax.nn.softmax(logits, axis=-1)
+    gate = jnp.sum(prob * mark, axis=-1, keepdims=True)
+    pre = dot_plain(rows_x, both_in)
+    cdf = 0.5 * (1.0 + lax.erf(pre * 0.7071067811865476))
+    slope = cdf + pre * jnp.exp(-0.5 * pre * pre) * 0.3989422804014327
+    act = (pre * cdf).astype(jnp.bfloat16)
+    dy_hidden = dot_cols(rows_dy, both_out)
+    gate_part = jnp.sum(act.astype(jnp.float32) * dy_hidden, axis=-1, keepdims=True)
+    pre_grad = (gate * dy_hidden * slope).astype(jnp.bfloat16)
+    gated = (gate * act.astype(jnp.float32)).astype(jnp.bfloat16)
+
+    share_hi, share_lo = split_bf16((gate_part * gate) * (mark - prob), 2)
 
     tiles = width // 128
     deal = experts * tiles // groups

time: 160 us -> 151 us (0.944)
  waiting for transfers between devices: 50.9 us -> 48 us
  local copies, waits for them, and re-layouts: 6.33 us -> 4.36 us
  other arithmetic: 9.57 us -> 7.8 us
    ppermute x4, waiting for transfers between devices: 11.6 us -> 8.22 us  [grads(): up = lax.ppermute(up, 'dp', [(i, (i + 2) % groups) for i in range(groups)])]
    ppermute x3, starting transfers between devices: 20.3 us -> 17.7 us  [grads(): lax.ppermute(down, 'dp', [(i, (i - 2) % groups) for i in range(groups)])]
    ppermute x4, starting transfers between devices: 7.67 us -> 9.74 us  [grads(): up = lax.ppermute(up, 'dp', [(i, (i + 2) % groups) for i in range(groups)])]
    dot_general x4 -> x3, matrix products: 3.37 us -> 1.79 us  [dot_cols(): lax.dot_general(left, right, (((1,), (1,)), ((), ())), preferred_element_...]
    dot_general x9 -> x7, matrix products: 4.49 us -> 4.53 us  [dot_plain(): return jnp.dot(left, right, preferred_element_type=jnp.float32)]
where the time goes in v4:
time: 151 us; the launch traced here: 150 us
  starting transfers between devices  72.5 us (48%)
  waiting for transfers between devices  48 us (32%)
  matrix products  16.1 us (11%)
  other arithmetic  7.8 us (5%)
  local copies, waits for them, and re-layouts  4.36 us (3%)
    all_to_all x1, waiting for transfers between devices, grads(): lax.all_to_all(rows, 'dp', split_axis=0, concat_axis=0, axis_index_groups...  19.1 us
    ppermute x3, starting transfers between devices, grads(): lax.ppermute(down, 'dp', [(i, (i - 2) % groups) for i in range(groups)])  17.7 us
    all_to_all x1, starting transfers between devices, grads(): lax.all_to_all(send, 'expert', split_axis=0, concat_axis=0, tiled=True)  10.5 us
    dot_general x8, matrix products, dot_rows(): lax.dot_general(left, right, (((0,), (0,)), ((), ())), preferred_element_...  9.75 us
    ppermute x4, starting transfers between devices, grads(): up = lax.ppermute(up, 'dp', [(i, (i + 2) % groups) for i in range(groups)])  9.74 us
    ppermute x1, starting transfers between devices, grads(): lax.ppermute(dealt(1 - core).astype(jnp.bfloat16), 'dp', swap)  9.19 us
    ppermute x4, waiting for transfers between devices, grads(): up = lax.ppermute(up, 'dp', [(i, (i + 2) % groups) for i in range(groups)])  8.22 us
    all_to_all x1, waiting for transfers between devices, grads(): lax.all_to_all(router_rows, 'dp', split_axis=0, concat_axis=0, tiled=True)  7.42 us
  transfers between devices with their start and end apart: 16, of which 8 were waited for; matrix products, arithmetic and copies ran while one was open for 11% of the time, Pallas kernels for 0%

profile of v4, /device:TPU:1, one launch (start us, length us, event | category | flops | bytes accessed | tf_op | source)
XLA Modules:
  0.0 150.0 jit_solution(7412911786645966935)
XLA Ops:
  0.7 0.9 fusion.68
  1.8 0.7 maximum_convert_fusion
  2.7 0.3 fusion.54
  3.0 1.4 fusion.6
  4.5 0.9 reshape.220
  5.3 10.5 %all-to-all-start = ((bf16[32,4,1664]{2,1,0:T(4,128)(2,1)}), bf16[32,4,1664]{2,1,0:T(4,128)(2,1)S(1)}, u32[]{:S(2)}, u32[]{:S(2)}) async-start(bf16[32,4,1664]{2,1,0:T(4,128)(2,1)} %reshape.220), calls=%async_computation | async-start | bytes 851968 | tf_op jit(solution)/shard_map/all_to_all | solution.py:67
  15.8 2.9 %collective-permute-start.7 = (bf16[1664,256]{1,0:T(8,128)(2,1)S(1)}, bf16[1664,256]{1,0:T(8,128)(2,1)}, u32[]{:S(2)}, u32[]{:S(2)}) collective-permute-start(bf16[1664,256]{1,0:T(8,128)(2,1)S(1)} %bitcast.124), channel_id=1, source_target_pairs={{0,32},{32,0},{64,96},{96,64},{128,160},{160,128},{192,224},{224,1... | collective-permute-start | bytes 2555912 | tf_op jit(solution)/shard_map/ppermute | solution.py:79
  18.7 1.9 %collective-permute-start.8 = (bf16[256,1664]{1,0:T(8,128)(2,1)}, bf16[256,1664]{1,0:T(8,128)(2,1)}, u32[]{:S(2)}, u32[]{:S(2)}) collective-permute-start(bf16[256,1664]{1,0:T(8,128)(2,1)} %bitcast.23), channel_id=1, source_target_pairs={{0,32},{32,0},{64,96},{96,64},{128,160},{160,128},{192,224},{224,1... | collective-permute-start | bytes 2555912 | tf_op jit(solution)/shard_map/ppermute | solution.py:80
  20.6 0.7 and_select_fusion.7
  21.4 0.8 broadcast_add_fusion
  22.5 5.7 %all-to-all-done = bf16[32,4,1664]{2,1,0:T(4,128)(2,1)S(1)} async-done(((bf16[32,4,1664]{2,1,0:T(4,128)(2,1)}), bf16[32,4,1664]{2,1,0:T(4,128)(2,1)S(1)}, u32[]{:S(2)}, u32[]{:S(2)}) %all-to-all-start) | async-done | bytes 426016 | tf_op jit(solution)/shard_map/all_to_all | solution.py:67
  28.5 4.0 %collective-permute-start = (bf16[64,1664]{1,0:T(8,128)(2,1)S(1)}, bf16[64,1664]{1,0:T(8,128)(2,1)S(1)}, u32[]{:S(2)}, u32[]{:S(2)}) collective-permute-start(bf16[64,1664]{1,0:T(8,128)(2,1)S(1)} %convolution_convert_fusion.3), channel_id=1, source_target_pairs={{0,64},{32,96},{64,128},{96,160},{128,192},{160,224},{192,256},{22... | collective-permute-start | bytes 638984 | tf_op jit(solution)/shard_map/ppermute | solution.py:96
  32.5 8.6 %collective-permute-start.1 = (bf16[64,1664]{1,0:T(8,128)(2,1)S(1)}, bf16[64,1664]{1,0:T(8,128)(2,1)S(1)}, u32[]{:S(2)}, u32[]{:S(2)}) collective-permute-start(bf16[64,1664]{1,0:T(8,128)(2,1)S(1)} %convolution_convert_fusion.3), channel_id=1, source_target_pairs={{0,448},{32,480},{64,0},{96,32},{128,64},{160,96},{192,128},{224,1... | collective-permute-start | bytes 638984 | tf_op jit(solution)/shard_map/ppermute | solution.py:99
  41.3 1.3 pad_maximum_fusion
  42.6 1.5 %pad_maximum_fusion.1 = bf16[512,1664]{1,0:T(8,128)(2,1)S(1)} fusion(bf16[256,1664]{1,0:T(8,128)(2,1)} %collective-permute-done.8, bf16[256,1664]{1,0:T(8,128)(2,1)} %bitcast.23), kind=kLoop, calls=%fused_computation.20 | loop fusion | flops 3407872 | bytes 3407872 | tf_op jit(solution)/shard_map/concatenate | solution.py:82
  44.2 1.9 %collective-permute-start.2 = (bf16[64,1664]{1,0:T(8,128)(2,1)S(1)}, bf16[64,1664]{1,0:T(8,128)(2,1)S(1)}, u32[]{:S(2)}, u32[]{:S(2)}) collective-permute-start(bf16[64,1664]{1,0:T(8,128)(2,1)S(1)} %collective-permute-done), channel_id=1, source_target_pairs={{0,64},{32,96},{64,128},{96,160},{128,192},{160,224},{192,256},{22... | collective-permute-start | bytes 638984 | tf_op jit(solution)/shard_map/ppermute | solution.py:96
  46.1 4.6 %collective-permute-start.3 = (bf16[64,1664]{1,0:T(8,128)(2,1)S(1)}, bf16[64,1664]{1,0:T(8,128)(2,1)S(1)}, u32[]{:S(2)}, u32[]{:S(2)}) collective-permute-start(bf16[64,1664]{1,0:T(8,128)(2,1)S(1)} %collective-permute-done.1), channel_id=1, source_target_pairs={{0,448},{32,480},{64,0},{96,32},{128,64},{160,96},{192,128},{224,1... | collective-permute-start | bytes 638984 | tf_op jit(solution)/shard_map/ppermute | solution.py:99
  50.8 1.2 collective-permute-done.2
  52.0 1.9 %collective-permute-start.4 = (bf16[64,1664]{1,0:T(8,128)(2,1)S(1)}, bf16[64,1664]{1,0:T(8,128)(2,1)S(1)}, u32[]{:S(2)}, u32[]{:S(2)}) collective-permute-start(bf16[64,1664]{1,0:T(8,128)(2,1)S(1)} %collective-permute-done.2), channel_id=1, source_target_pairs={{0,64},{32,96},{64,128},{96,160},{128,192},{160,224},{192,256},{22... | collective-permute-start | bytes 638984 | tf_op jit(solution)/shard_map/ppermute | solution.py:96
  53.9 4.6 %collective-permute-start.5 = (bf16[64,1664]{1,0:T(8,128)(2,1)S(1)}, bf16[64,1664]{1,0:T(8,128)(2,1)S(1)}, u32[]{:S(2)}, u32[]{:S(2)}) collective-permute-start(bf16[64,1664]{1,0:T(8,128)(2,1)S(1)} %collective-permute-done.3), channel_id=1, source_target_pairs={{0,448},{32,480},{64,0},{96,32},{128,64},{160,96},{192,128},{224,1... | collective-permute-start | bytes 638984 | tf_op jit(solution)/shard_map/ppermute | solution.py:99
  58.6 1.2 collective-permute-done.4
  59.8 1.9 %collective-permute-start.6 = (bf16[64,1664]{1,0:T(8,128)(2,1)S(1)}, bf16[64,1664]{1,0:T(8,128)(2,1)S(1)}, u32[]{:S(2)}, u32[]{:S(2)}) collective-permute-start(bf16[64,1664]{1,0:T(8,128)(2,1)S(1)} %collective-permute-done.4), channel_id=1, source_target_pairs={{0,64},{32,96},{64,128},{96,160},{128,192},{160,224},{192,256},{22... | collective-permute-start | bytes 638984 | tf_op jit(solution)/shard_map/ppermute | solution.py:96
  61.8 5.8 %collective-permute-done.6 = bf16[64,1664]{1,0:T(8,128)(2,1)S(1)} collective-permute-done((bf16[64,1664]{1,0:T(8,128)(2,1)S(1)}, bf16[64,1664]{1,0:T(8,128)(2,1)S(1)}, u32[]{:S(2)}, u32[]{:S(2)}) %collective-permute-start.6) | collective-permute-done | bytes 213024 | tf_op jit(solution)/shard_map/ppermute | solution.py:96
  67.6 0.4 fusion.20
  68.0 0.7 fusion.82
  68.8 1.6 %fusion.10 = (bf16[256,512]{1,0:T(8,128)(2,1)}, bf16[256,512]{1,0:T(8,128)(2,1)S(1)}, bf16[256,512]{1,0:T(8,128)(2,1)S(1)}) fusion(f32[256]{0:T(256)S(1)} %multiply_reduce_fusion, f32[256,512]{1,0:T(8,128)S(1)} %fusion.82, bf16[256,1664]{1,0:T(8,128)(2,1)S(1)} %bitcast.115, bf16[1664,512]{1,0:T(8,128)(2,1)S(1)} %pad_maximum_fusion), kind=kOutput, calls=%fused_computation.28 | convolution fusion | flops 438304768 | bytes 3867648 | tf_op jit(solution)/shard_map/dot_general | solution.py:23
  70.9 0.4 fusion.23
  72.0 9.2 %collective-permute-start.9 = (bf16[256,128]{1,0:T(8,128)(2,1)S(1)}, bf16[256,128]{1,0:T(8,128)(2,1)S(1)}, u32[]{:S(2)}, u32[]{:S(2)}) collective-permute-start(bf16[256,128]{1,0:T(8,128)(2,1)S(1)} %convolution_convert_fusion.4), channel_id=1, source_target_pairs={{0,32},{32,0},{64,96},{96,64},{128,160},{160,128},{192,224},{224,1... | collective-permute-start | bytes 196616 | tf_op jit(solution)/shard_map/ppermute | solution.py:145
  81.2 0.7 fusion.2
  82.4 1.0 pad_maximum_fusion.2
  83.4 4.4 %all-to-all-start.1 = ((bf16[8,32,1792]{2,1,0:T(8,128)(2,1)}), bf16[8,32,1792]{2,1,0:T(8,128)(2,1)S(1)}, u32[]{:S(2)}, u32[]{:S(2)}) async-start(bf16[8,32,1792]{2,1,0:T(8,128)(2,1)} %bitcast.24), calls=%async_computation.1 | async-start | bytes 1835008 | tf_op jit(solution)/shard_map/all_to_all | solution.py:152
  87.8 1.3 convolution_convert_fusion.1
  89.2 2.5 %collective-permute-start.10 = (bf16[1664,256]{1,0:T(8,128)(2,1)}, bf16[1664,256]{1,0:T(8,128)(2,1)}, u32[]{:S(2)}, u32[]{:S(2)}) collective-permute-start(bf16[1664,256]{1,0:T(8,128)(2,1)} %convolution_convert_fusion.1), channel_id=1, source_target_pairs={{0,32},{32,0},{64,96},{96,64},{128,160},{160,128},{192,224},{224,1... | collective-permute-start | bytes 2555912 | tf_op jit(solution)/shard_map/ppermute | solution.py:165
  91.7 1.3 convolution_convert_fusion
  93.1 1.9 %collective-permute-start.11 = (bf16[256,1664]{1,0:T(8,128)(2,1)}, bf16[256,1664]{1,0:T(8,128)(2,1)}, u32[]{:S(2)}, u32[]{:S(2)}) collective-permute-start(bf16[256,1664]{1,0:T(8,128)(2,1)} %convolution_convert_fusion), channel_id=1, source_target_pairs={{0,32},{32,0},{64,96},{96,64},{128,160},{160,128},{192,224},{224,1... | collective-permute-start | bytes 2555912 | tf_op jit(solution)/shard_map/ppermute | solution.py:166
  95.0 19.1 %all-to-all-done.1 = bf16[8,32,1792]{2,1,0:T(8,128)(2,1)S(1)} async-done(((bf16[8,32,1792]{2,1,0:T(8,128)(2,1)}), bf16[8,32,1792]{2,1,0:T(8,128)(2,1)S(1)}, u32[]{:S(2)}, u32[]{:S(2)}) %all-to-all-start.1) | async-done | bytes 917536 | tf_op jit(solution)/shard_map/all_to_all | solution.py:152
  114.2 0.4 fusion.7
  114.7 0.9 reshape.226
  115.5 5.2 %all-to-all-start.2 = ((bf16[32,4,1664]{2,1,0:T(4,128)(2,1)}), bf16[32,4,1664]{2,1,0:T(4,128)(2,1)S(1)}, u32[]{:S(2)}, u32[]{:S(2)}) async-start(bf16[32,4,1664]{2,1,0:T(4,128)(2,1)} %reshape.226), calls=%async_computation.2 | async-start | bytes 851968 | tf_op jit(solution)/shard_map/all_to_all | solution.py:176
  120.8 2.5 %fusion.4 = bf16[1,256,1664]{2,1,0:T(8,128)(2,1)} fusion(bf16[256,1664]{1,0:T(8,128)(2,1)S(1)} %bitcast.122, bf16[256,1664]{1,0:T(8,128)(2,1)} %collective-permute-done.11, bf16[256,512]{1,0:T(8,128)(2,1)S(1)} %copy-done.3), kind=kOutput, calls=%fused_computation.11 | convolution fusion | flops 219381760 | bytes 2686976 | tf_op jit(solution)/shard_map/dot_general | solution.py:11
  123.3 2.5 %fusion.5 = bf16[1,1664,256]{2,1,0:T(8,128)(2,1)} fusion(bf16[256,1664]{1,0:T(8,128)(2,1)S(1)} %bitcast.119, bf16[1664,256]{1,0:T(8,128)(2,1)} %collective-permute-done.10, bf16[256,512]{1,0:T(8,128)(2,1)S(1)} %get-tuple-element.17), kind=kOutput, calls=%fused_computation.12 | convolution fusion | flops 219381760 | bytes 2686976 | tf_op jit(solution)/shard_map/dot_general | solution.py:11
  125.8 7.4 %all-to-all-done.2 = bf16[32,4,1664]{2,1,0:T(4,128)(2,1)S(1)} async-done(((bf16[32,4,1664]{2,1,0:T(4,128)(2,1)}), bf16[32,4,1664]{2,1,0:T(4,128)(2,1)S(1)}, u32[]{:S(2)}, u32[]{:S(2)}) %all-to-all-start.2) | async-done | bytes 426016 | tf_op jit(solution)/shard_map/all_to_all | solution.py:176
  133.1 0.3 slice_reduce_fusion
  133.4 0.7 broadcast_in_dim.143
  134.1 6.5 %all-to-all-start.3 = ((bf16[16,2,1664]{2,1,0:T(2,128)(2,1)}), bf16[16,2,1664]{2,1,0:T(2,128)(2,1)S(1)}, u32[]{:S(2)}, u32[]{:S(2)}) async-start(bf16[16,2,1664]{2,1,0:T(2,128)(2,1)} %broadcast_in_dim.143), calls=%async_computation.3 | async-start | bytes 212992 | tf_op jit(solution)/shard_map/all_to_all | solution.py:187
  140.7 1.1 convolution_convert_fusion.2
  141.9 7.4 %all-to-all-done.3 = bf16[16,2,1664]{2,1,0:T(2,128)(2,1)S(1)} async-done(((bf16[16,2,1664]{2,1,0:T(2,128)(2,1)}), bf16[16,2,1664]{2,1,0:T(2,128)(2,1)S(1)}, u32[]{:S(2)}, u32[]{:S(2)}) %all-to-all-start.3) | async-done | bytes 106528 | tf_op jit(solution)/shard_map/all_to_all | solution.py:187
  149.3 0.7 reshape.228
  (75 shorter events, 3.4 us)
Async XLA Ops:
  0.6 2.0 %copy-start = (bf16[128,1664]{1,0:T(8,128)(2,1)S(1)}, bf16[128,1664]{1,0:T(8,128)(2,1)}, u32[]{:S(2)}) copy-start(bf16[128,1664]{1,0:T(8,128)(2,1)} %param.7) | copy-start | bytes 1277956
  3.0 12.8 %copy-start.1 = (bf16[1,1664,256]{2,1,0:T(8,128)(2,1)S(1)}, bf16[1,1664,256]{2,1,0:T(8,128)(2,1)}, u32[]{:S(2)}) copy-start(bf16[1,1664,256]{2,1,0:T(8,128)(2,1)} %param.12) | copy-start | bytes 2555908
  4.5 18.0 %copy-start.4 = (f32[1664,32]{0,1:T(8,128)S(1)}, f32[1664,32]{0,1:T(8,128)}, u32[]{:S(2)}) copy-start(f32[1664,32]{0,1:T(8,128)} %param.11) | copy-start | bytes 638980
  5.3 22.8 %all-to-all-start = ((bf16[32,4,1664]{2,1,0:T(4,128)(2,1)}), bf16[32,4,1664]{2,1,0:T(4,128)(2,1)S(1)}, u32[]{:S(2)}, u32[]{:S(2)}) async-start(bf16[32,4,1664]{2,1,0:T(4,128)(2,1)} %reshape.220), calls=%async_computation | async-start | bytes 851968 | tf_op jit(solution)/shard_map/all_to_all | solution.py:67
  15.8 25.5 %collective-permute-start.7 = (bf16[1664,256]{1,0:T(8,128)(2,1)S(1)}, bf16[1664,256]{1,0:T(8,128)(2,1)}, u32[]{:S(2)}, u32[]{:S(2)}) collective-permute-start(bf16[1664,256]{1,0:T(8,128)(2,1)S(1)} %bitcast.124), channel_id=1, source_target_pairs={{0,32},{32,0},{64,96},{96,64},{128,160},{160,128},{192,224},{224,1... | collective-permute-start | bytes 2555912 | tf_op jit(solution)/shard_map/ppermute | solution.py:79
  18.7 23.9 %collective-permute-start.8 = (bf16[256,1664]{1,0:T(8,128)(2,1)}, bf16[256,1664]{1,0:T(8,128)(2,1)}, u32[]{:S(2)}, u32[]{:S(2)}) collective-permute-start(bf16[256,1664]{1,0:T(8,128)(2,1)} %bitcast.23), channel_id=1, source_target_pairs={{0,32},{32,0},{64,96},{96,64},{128,160},{160,128},{192,224},{224,1... | collective-permute-start | bytes 2555912 | tf_op jit(solution)/shard_map/ppermute | solution.py:80
  28.5 15.6 %collective-permute-start = (bf16[64,1664]{1,0:T(8,128)(2,1)S(1)}, bf16[64,1664]{1,0:T(8,128)(2,1)S(1)}, u32[]{:S(2)}, u32[]{:S(2)}) collective-permute-start(bf16[64,1664]{1,0:T(8,128)(2,1)S(1)} %convolution_convert_fusion.3), channel_id=1, source_target_pairs={{0,64},{32,96},{64,128},{96,160},{128,192},{160,224},{192,256},{22... | collective-permute-start | bytes 638984 | tf_op jit(solution)/shard_map/ppermute | solution.py:96
  32.5 13.6 %collective-permute-start.1 = (bf16[64,1664]{1,0:T(8,128)(2,1)S(1)}, bf16[64,1664]{1,0:T(8,128)(2,1)S(1)}, u32[]{:S(2)}, u32[]{:S(2)}) collective-permute-start(bf16[64,1664]{1,0:T(8,128)(2,1)S(1)} %convolution_convert_fusion.3), channel_id=1, source_target_pairs={{0,448},{32,480},{64,0},{96,32},{128,64},{160,96},{192,128},{224,1... | collective-permute-start | bytes 638984 | tf_op jit(solution)/shard_map/ppermute | solution.py:99
  44.2 7.8 %collective-permute-start.2 = (bf16[64,1664]{1,0:T(8,128)(2,1)S(1)}, bf16[64,1664]{1,0:T(8,128)(2,1)S(1)}, u32[]{:S(2)}, u32[]{:S(2)}) collective-permute-start(bf16[64,1664]{1,0:T(8,128)(2,1)S(1)} %collective-permute-done), channel_id=1, source_target_pairs={{0,64},{32,96},{64,128},{96,160},{128,192},{160,224},{192,256},{22... | collective-permute-start | bytes 638984 | tf_op jit(solution)/shard_map/ppermute | solution.py:96
  46.1 7.8 %collective-permute-start.3 = (bf16[64,1664]{1,0:T(8,128)(2,1)S(1)}, bf16[64,1664]{1,0:T(8,128)(2,1)S(1)}, u32[]{:S(2)}, u32[]{:S(2)}) collective-permute-start(bf16[64,1664]{1,0:T(8,128)(2,1)S(1)} %collective-permute-done.1), channel_id=1, source_target_pairs={{0,448},{32,480},{64,0},{96,32},{128,64},{160,96},{192,128},{224,1... | collective-permute-start | bytes 638984 | tf_op jit(solution)/shard_map/ppermute | solution.py:99
  52.0 7.8 %collective-permute-start.4 = (bf16[64,1664]{1,0:T(8,128)(2,1)S(1)}, bf16[64,1664]{1,0:T(8,128)(2,1)S(1)}, u32[]{:S(2)}, u32[]{:S(2)}) collective-permute-start(bf16[64,1664]{1,0:T(8,128)(2,1)S(1)} %collective-permute-done.2), channel_id=1, source_target_pairs={{0,64},{32,96},{64,128},{96,160},{128,192},{160,224},{192,256},{22... | collective-permute-start | bytes 638984 | tf_op jit(solution)/shard_map/ppermute | solution.py:96
  53.9 7.8 %collective-permute-start.5 = (bf16[64,1664]{1,0:T(8,128)(2,1)S(1)}, bf16[64,1664]{1,0:T(8,128)(2,1)S(1)}, u32[]{:S(2)}, u32[]{:S(2)}) collective-permute-start(bf16[64,1664]{1,0:T(8,128)(2,1)S(1)} %collective-permute-done.3), channel_id=1, source_target_pairs={{0,448},{32,480},{64,0},{96,32},{128,64},{160,96},{192,128},{224,1... | collective-permute-start | bytes 638984 | tf_op jit(solution)/shard_map/ppermute | solution.py:99
  59.8 7.8 %collective-permute-start.6 = (bf16[64,1664]{1,0:T(8,128)(2,1)S(1)}, bf16[64,1664]{1,0:T(8,128)(2,1)S(1)}, u32[]{:S(2)}, u32[]{:S(2)}) collective-permute-start(bf16[64,1664]{1,0:T(8,128)(2,1)S(1)} %collective-permute-done.4), channel_id=1, source_target_pairs={{0,64},{32,96},{64,128},{96,160},{128,192},{160,224},{192,256},{22... | collective-permute-start | bytes 638984 | tf_op jit(solution)/shard_map/ppermute | solution.py:96
  72.0 10.1 %collective-permute-start.9 = (bf16[256,128]{1,0:T(8,128)(2,1)S(1)}, bf16[256,128]{1,0:T(8,128)(2,1)S(1)}, u32[]{:S(2)}, u32[]{:S(2)}) collective-permute-start(bf16[256,128]{1,0:T(8,128)(2,1)S(1)} %convolution_convert_fusion.4), channel_id=1, source_target_pairs={{0,32},{32,0},{64,96},{96,64},{128,160},{160,128},{192,224},{224,1... | collective-permute-start | bytes 196616 | tf_op jit(solution)/shard_map/ppermute | solution.py:145
  83.4 30.8 %all-to-all-start.1 = ((bf16[8,32,1792]{2,1,0:T(8,128)(2,1)}), bf16[8,32,1792]{2,1,0:T(8,128)(2,1)S(1)}, u32[]{:S(2)}, u32[]{:S(2)}) async-start(bf16[8,32,1792]{2,1,0:T(8,128)(2,1)} %bitcast.24), calls=%async_computation.1 | async-start | bytes 1835008 | tf_op jit(solution)/shard_map/all_to_all | solution.py:152
  87.8 3.9 %copy-start.2 = (bf16[256,512]{1,0:T(8,128)(2,1)S(1)}, bf16[256,512]{1,0:T(8,128)(2,1)}, u32[]{:S(2)}) copy-start(bf16[256,512]{1,0:T(8,128)(2,1)} %get-tuple-element.11) | copy-start | bytes 786436
  89.2 34.1 %collective-permute-start.10 = (bf16[1664,256]{1,0:T(8,128)(2,1)}, bf16[1664,256]{1,0:T(8,128)(2,1)}, u32[]{:S(2)}, u32[]{:S(2)}) collective-permute-start(bf16[1664,256]{1,0:T(8,128)(2,1)} %convolution_convert_fusion.1), channel_id=1, source_target_pairs={{0,32},{32,0},{64,96},{96,64},{128,160},{160,128},{192,224},{224,1... | collective-permute-start | bytes 2555912 | tf_op jit(solution)/shard_map/ppermute | solution.py:165
  93.1 27.7 %collective-permute-start.11 = (bf16[256,1664]{1,0:T(8,128)(2,1)}, bf16[256,1664]{1,0:T(8,128)(2,1)}, u32[]{:S(2)}, u32[]{:S(2)}) collective-permute-start(bf16[256,1664]{1,0:T(8,128)(2,1)} %convolution_convert_fusion), channel_id=1, source_target_pairs={{0,32},{32,0},{64,96},{96,64},{128,160},{160,128},{192,224},{224,1... | collective-permute-start | bytes 2555912 | tf_op jit(solution)/shard_map/ppermute | solution.py:166
  114.2 6.5 %copy-start.3 = (bf16[256,512]{1,0:T(8,128)(2,1)S(1)}, bf16[256,512]{1,0:T(8,128)(2,1)}, u32[]{:S(2)}) copy-start(bf16[256,512]{1,0:T(8,128)(2,1)} %get-tuple-element.11) | copy-start | bytes 786436
  115.5 17.6 %all-to-all-start.2 = ((bf16[32,4,1664]{2,1,0:T(4,128)(2,1)}), bf16[32,4,1664]{2,1,0:T(4,128)(2,1)S(1)}, u32[]{:S(2)}, u32[]{:S(2)}) async-start(bf16[32,4,1664]{2,1,0:T(4,128)(2,1)} %reshape.226), calls=%async_computation.2 | async-start | bytes 851968 | tf_op jit(solution)/shard_map/all_to_all | solution.py:176
  134.1 15.2 %all-to-all-start.3 = ((bf16[16,2,1664]{2,1,0:T(2,128)(2,1)}), bf16[16,2,1664]{2,1,0:T(2,128)(2,1)S(1)}, u32[]{:S(2)}, u32[]{:S(2)}) async-start(bf16[16,2,1664]{2,1,0:T(2,128)(2,1)} %broadcast_in_dim.143), calls=%async_computation.3 | async-start | bytes 212992 | tf_op jit(solution)/shard_map/all_to_all | solution.py:187
